TPU v7x, 512 devices: a whole 4x4x16 slice. The times are simulated.
512 devices in a mesh: dp: 512 (over z, x, y, core).
Axes of the slice: x: 4, y: 4, z: 16, core: 2. Of those that a mesh axis runs over, the one named last changes fastest.
Arguments:
- inputs: bfloat16 [2048, 199, 512], P('dp'), may hold values from -6 to 6
- weights: bfloat16 [2, 262144], replicated, may hold values from -0.1875 to 0.1875
- ln_gain: float32 [512], replicated, may hold values from 0.45 to 2.16
- ln_bias: float32 [512], replicated, may hold values from -3 to 3
- projection: bfloat16 [512, 1024], replicated, may hold values from -0.25 to 0.25
- targets: float32 [2048, 1024], P('dp'), may hold values from -6 to 6
- master: float32 [2, 262144], P(None, 'dp'), may hold values from -0.006 to 0.006
- first_moment: float32 [2, 262144], P(None, 'dp'), may hold values from -0.0006 to 0.0006
- second_moment: float32 [2, 262144], P(None, 'dp'), may hold values from 1e-11 to 1e-08
Outputs:
- input_grad: bfloat16 [2048, 199, 512], P('dp')
- update: float32 [2, 262144], P(None, 'dp')
- new_master: float32 [2, 262144], P(None, 'dp')
- new_first: float32 [2, 262144], P(None, 'dp')
- new_second: float32 [2, 262144], P(None, 'dp')
- new_weights: bfloat16 [2, 262144], replicated
All inputs are finite; a program needn't handle non-finite values.
Results may differ from a plain program's by a relative error of at most 0.006.
Values may be sent and summed in bfloat16 or wider, within the bound.
No kernel may reach another device: no remote copies, remote signals or barrier semaphores. Data moves between devices by JAX's collectives and lax.ppermute only.
A program may use at most 64 MiB of HBM per device.

v0:
```python
import jax
import jax.numpy as jnp
from jax import lax
from jax.sharding import PartitionSpec as P


def norm_act(pre, gain, bias):
    center = pre - jnp.mean(pre, axis=-1, keepdims=True)
    spread = jnp.mean(center * center, axis=-1, keepdims=True)
    normed = center * lax.rsqrt(spread + 1e-05)
    return jax.nn.gelu(normed * gain + bias, approximate=False)


def local_pass(inputs, weights, ln_gain, ln_bias, projection, targets):
    clips, frames_in, chans = inputs.shape
    taps = weights.shape[0]
    frames_out = (frames_in - taps) // taps + 1
    windows = inputs[:, : frames_out * taps].reshape(clips, frames_out, taps, chans)
    kernel = weights.reshape(taps, chans, chans)
    pre = jnp.einsum("bfki,koi->bfo", windows, kernel, preferred_element_type=jnp.float32)
    act, pull = jax.vjp(lambda value: norm_act(value, ln_gain, ln_bias), pre)
    pooled = jnp.mean(act, axis=1).astype(jnp.bfloat16)
    predicted = jnp.dot(pooled, projection, preferred_element_type=jnp.float32)
    miss = (predicted - targets).astype(jnp.bfloat16)
    back = lax.dot_general(
        miss, projection, (((1,), (1,)), ((), ())), preferred_element_type=jnp.float32
    )
    upstream = jnp.broadcast_to(back[:, None, :] / frames_out, act.shape)
    dpre = pull(upstream)[0].astype(jnp.bfloat16)
    dwin = jnp.einsum("bfo,koi->bfki", dpre, kernel, preferred_element_type=jnp.float32).astype(
        jnp.bfloat16
    )
    dinput = dwin.reshape(clips, frames_out * taps, chans)
    tail = jnp.zeros((clips, frames_in - frames_out * taps, chans), jnp.bfloat16)
    return (windows, dpre, jnp.concatenate([dinput, tail], axis=1))


def body(
    inputs, weights, ln_gain, ln_bias, projection, targets, master, first_moment, second_moment
):
    windows, dpre, input_grad = local_pass(inputs, weights, ln_gain, ln_bias, projection, targets)
    taps = weights.shape[0]
    term = jnp.einsum("bfo,bfki->koi", dpre, windows, preferred_element_type=jnp.float32)
    grad = lax.psum_scatter(term.reshape(taps, -1), "dp", scatter_dimension=1, tiled=True)
    squares = lax.psum(jnp.sum(grad * grad), "dp")
    scale = jnp.minimum(1.0, 1.0 / (jnp.sqrt(squares) + 1e-06))
    clipped = scale * grad
    new_first = 0.9 * first_moment + 0.1 * clipped
    new_second = 0.999 * second_moment + 0.001 * clipped * clipped
    update = new_first / (1.0 - 0.9**20) / (jnp.sqrt(new_second / (1.0 - 0.999**20)) + 1e-08)
    new_master = master - 0.0001 * (update + 0.01 * master)
    new_weights = lax.all_gather(new_master.astype(jnp.bfloat16), "dp", axis=1, tiled=True)
    return (input_grad, update, new_master, new_first, new_second, new_weights)


def solution(mesh):
    return jax.shard_map(
        body,
        mesh=mesh,
        in_specs=(
            P("dp", None, None),
            P(),
            P(),
            P(),
            P(),
            P("dp", None),
            P(None, "dp"),
            P(None, "dp"),
            P(None, "dp"),
        ),
        out_specs=(
            P("dp", None, None),
            P(None, "dp"),
            P(None, "dp"),
            P(None, "dp"),
            P(None, "dp"),
            P(),
        ),
        check_vma=False,
    )
```

profile of v0, /device:TPU:1, one launch (start us, length us, event | category | flops | bytes accessed | tf_op | source)
XLA Modules:
  0.0 786.2 jit_solution(7399412350724682430)
XLA Ops:
  7.2 0.0 copy-start
  7.2 0.0 all-reduce.4.cloned.1.call-start
  7.2 1.5 slice.3
  8.7 0.0 copy-start.1
  8.7 0.0 copy-start.5
  8.8 0.0 copy-start.6
  8.8 2.3 fusion.26
  11.1 0.3 multiply_reduce_fusion.2
  11.4 2.2 multiply_reduce_fusion.1
  13.6 0.0 copy-done
  13.6 0.0 copy-done.7
  13.6 0.5 broadcast_multiply_fusion
  14.1 0.7 multiply_reduce_fusion
  14.9 0.8 fusion.24
  15.7 0.0 copy-start.3
  15.8 0.9 copy-done.3
  16.6 0.9 convolution_bitcast_fusion
  17.5 2.9 copy.28
  20.5 0.0 copy-start.11
  20.5 0.0 all-reduce.4.cloned.1.call-update
  20.5 0.0 all-gather.2.cloned.1.call-start
  20.6 487.3 %all-reduce.4.cloned.1.call-done = f32[2,262144]{1,0:T(2,128)} async-done(((f32[2,262144]{1,0:T(2,128)}), f32[2,262144]{1,0:T(2,128)}) %all-reduce.4.cloned.1.call-update) | async-done | bytes 2097168
  507.8 1.3 multiply_reduce_fusion.3
  509.1 103.3 %psum.7 = f32[]{:T(128)} all-reduce(f32[]{:T(128)} %multiply_reduce_fusion.3), channel_id=1, replica_groups=mesh['dp'=512] {'dp'}, use_global_device_ids=true, to_apply=%region_7.0 | all-reduce | flops 1 | bytes 8 | tf_op jit(solution)/shard_map/psum | solution.py:45
  613.2 1.3 fusion.22
  614.5 0.0 all-gather.2.cloned.1.call-update
  614.5 0.0 copy-done.4
  614.6 0.7 convolution_convert_fusion
  615.2 0.6 copy.20
  615.9 1.2 concatenate.3
  617.1 159.7 %all-gather.2.cloned.1.call-done = bf16[2,262144]{1,0:T(2,128)(2,1)} async-done(((bf16[2,512]{1,0:T(2,128)(2,1)}), bf16[2,262144]{1,0:T(2,128)(2,1)}) %all-gather.2.cloned.1.call-update) | async-done | bytes 1048592 | tf_op jit(solution)/shard_map/all_gather | solution.py:52
  776.8 2.6 copy.47
  (18 shorter events, 0.1 us)
Async XLA Ops:
  7.2 6.5 copy-start
  7.2 500.6 %all-reduce.4.cloned.1.call-start = ((), (), s32[]{:S(2)}) async-start(), calls=%async_computation.1 | async-start | bytes 4194304
  8.7 2.6 copy-start.1
  8.7 2.6 copy-start.5
  8.8 2.6 copy-start.6
  11.1 2.6 copy-start.7
  14.1 2.5 copy-start.2
  15.7 0.9 copy-start.3
  20.5 592.7 %copy-start.8 = (f32[2,512]{1,0:T(2,128)S(1)}, f32[2,512]{1,0:T(2,128)}, u32[]{:S(2)}) copy-start(f32[2,512]{1,0:T(2,128)} %param.15) | copy-start | bytes 12292
  20.5 592.7 %copy-start.9 = (f32[2,512]{1,0:T(2,128)S(1)}, f32[2,512]{1,0:T(2,128)}, u32[]{:S(2)}) copy-start(f32[2,512]{1,0:T(2,128)} %param.16) | copy-start | bytes 12292
  20.5 592.7 %copy-start.10 = (f32[2,512]{1,0:T(2,128)S(1)}, f32[2,512]{1,0:T(2,128)}, u32[]{:S(2)}) copy-start(f32[2,512]{1,0:T(2,128)} %param.17) | copy-start | bytes 12292
  20.5 594.1 %copy-start.4 = (f32[4,99,512]{2,1,0:T(8,128)S(1)}, f32[4,99,512]{2,1,0:T(8,128)}, u32[]{:S(2)}) copy-start(f32[4,99,512]{2,1,0:T(8,128)} %copy-done.3) | copy-start | bytes 2433028
  20.5 594.1 %copy-start.11 = (bf16[2,262144]{1,0:T(2,128)(2,1)S(1)}, bf16[2,262144]{1,0:T(2,128)(2,1)}, u32[]{:S(2)}) copy-start(bf16[2,262144]{1,0:T(2,128)(2,1)} %param.10) | copy-start | bytes 3145732
  20.5 756.3 %all-gather.2.cloned.1.call-start = ((), (), s32[]{:S(2)}) async-start(), calls=%async_computation | async-start | bytes 1050624 | tf_op jit(solution)/shard_map/all_gather | solution.py:52
Sparse Core Ops, SparseCore 0:
  20.6 487.1 all-reduce.3
  614.7 162.0 all-gather.1
where the time goes:
time: 787 us; the launch traced here: 786 us
  waiting for transfers between devices  647 us (82%)
  blocking collectives  103 us (13%)
  between operations  15 us (2%)
  local copies, waits for them, and re-layouts  9.76 us (1%)
    unnamed x3, waiting for transfers between devices  487 us
    all_gather x1, waiting for transfers between devices, body(): lax.all_gather(new_master.astype(jnp.bfloat16), 'dp', axis=1, tiled=True)  160 us
    psum x1, blocking collectives, body(): squares = lax.psum(jnp.sum(grad * grad), 'dp')  103 us
  transfers between devices with their start and end apart: 2, of which 2 were waited for; matrix products, arithmetic and copies ran while one was open for 0% of the time, Pallas kernels for 0%

commit v1 on v0

--- a/solution.py
+++ b/solution.py
@@ -1,6 +1,7 @@
 import jax
 import jax.numpy as jnp
 from jax import lax
+from jax.sharding import Mesh
 from jax.sharding import PartitionSpec as P
 
 
@@ -35,45 +36,77 @@
     return (windows, dpre, jnp.concatenate([dinput, tail], axis=1))
 
 
+AXES = ("z", "x", "y", "core")
+PLANE = ("x", "y", "core")
+
+
+def exchange(value, axes):
+    return lax.all_to_all(value, axes, 0, 0, tiled=False)
+
+
+def spread(value, axes, count):
+    return exchange(jnp.broadcast_to(value[None], (count,) + value.shape), axes)
+
+
 def body(
     inputs, weights, ln_gain, ln_bias, projection, targets, master, first_moment, second_moment
 ):
+    depth, plane = lax.axis_size("z"), lax.axis_size(PLANE)
+    taps, width = weights.shape[0], ln_gain.shape[0]
+    f32, bf16 = jnp.float32, jnp.bfloat16
     windows, dpre, input_grad = local_pass(inputs, weights, ln_gain, ln_bias, projection, targets)
-    taps = weights.shape[0]
-    term = jnp.einsum("bfo,bfki->koi", dpre, windows, preferred_element_type=jnp.float32)
-    grad = lax.psum_scatter(term.reshape(taps, -1), "dp", scatter_dimension=1, tiled=True)
-    squares = lax.psum(jnp.sum(grad * grad), "dp")
+    term = jnp.einsum("bfo,bfki->koi", dpre, windows, preferred_element_type=f32).astype(bf16)
+    term = term.reshape(taps, depth, plane, width).transpose(2, 1, 0, 3)
+    part = jnp.sum(exchange(term, PLANE).astype(f32), axis=0).astype(bf16)
+    high = master.astype(bf16)
+    low = (master - high.astype(f32)).astype(bf16)
+    state = jnp.stack([high, low, first_moment.astype(bf16), second_moment.astype(bf16)])
+    packed = jnp.concatenate([part, state], axis=0)
+    column = spread(packed, "z", depth)
+    grad = jnp.sum(column[:, :depth].astype(f32), axis=0)
+    state = column[:, depth:].astype(f32)
+    piece = jnp.full((8, 128), jnp.sum(grad * grad), f32)
+    squares = jnp.sum(spread(piece, PLANE, plane)[:, 0, 0])
     scale = jnp.minimum(1.0, 1.0 / (jnp.sqrt(squares) + 1e-06))
-    clipped = scale * grad
-    new_first = 0.9 * first_moment + 0.1 * clipped
-    new_second = 0.999 * second_moment + 0.001 * clipped * clipped
-    update = new_first / (1.0 - 0.9**20) / (jnp.sqrt(new_second / (1.0 - 0.999**20)) + 1e-08)
-    new_master = master - 0.0001 * (update + 0.01 * master)
-    new_weights = lax.all_gather(new_master.astype(jnp.bfloat16), "dp", axis=1, tiled=True)
+
+    def advance(grad, master, first_moment, second_moment):
+        clipped = scale * grad
+        new_first = 0.9 * first_moment + 0.1 * clipped
+        new_second = 0.999 * second_moment + 0.001 * clipped * clipped
+        update = new_first / (1.0 - 0.9**20) / (jnp.sqrt(new_second / (1.0 - 0.999**20)) + 1e-08)
+        new_master = master - 0.0001 * (update + 0.01 * master)
+        return update, new_master, new_first, new_second
+
+    mine = lax.dynamic_index_in_dim(grad, lax.axis_index("z"), 0, keepdims=False)
+    update, new_master, new_first, new_second = advance(mine, master, first_moment, second_moment)
+    rows = advance(grad, state[:, 0] + state[:, 1], state[:, 2], state[:, 3])[1].astype(bf16)
+    whole = spread(rows, PLANE, plane)
+    new_weights = whole.transpose(2, 1, 0, 3).reshape(taps, -1)
     return (input_grad, update, new_master, new_first, new_second, new_weights)
 
 
 def solution(mesh):
+    grid = Mesh(mesh.devices.reshape(16, 4, 4, 2), AXES)
     return jax.shard_map(
         body,
-        mesh=mesh,
+        mesh=grid,
         in_specs=(
-            P("dp", None, None),
+            P(AXES, None, None),
             P(),
             P(),
             P(),
             P(),
-            P("dp", None),
-            P(None, "dp"),
-            P(None, "dp"),
-            P(None, "dp"),
+            P(AXES, None),
+            P(None, AXES),
+            P(None, AXES),
+            P(None, AXES),
         ),
         out_specs=(
-            P("dp", None, None),
-            P(None, "dp"),
-            P(None, "dp"),
-            P(None, "dp"),
-            P(None, "dp"),
+            P(AXES, None, None),
+            P(None, AXES),
+            P(None, AXES),
+            P(None, AXES),
+            P(None, AXES),
             P(),
         ),
         check_vma=False,

time: 787 us -> 129 us (0.16)
  waiting for transfers between devices: 647 us -> 37.1 us
  blocking collectives: 103 us -> 47.7 us
  starting transfers between devices: 0.08 us -> 20.5 us
  between operations: 15 us -> 1.7 us
    unnamed x3 -> x0, waiting for transfers between devices: 487 us -> none
    all_gather x1 -> x0, waiting for transfers between devices: 160 us -> none  [body(): lax.all_gather(new_master.astype(jnp.bfloat16), 'dp', axis=1, tiled=True)]
    psum x1 -> x0, blocking collectives: 103 us -> none  [body(): squares = lax.psum(jnp.sum(grad * grad), 'dp')]
    all_to_all x0 -> x1, blocking collectives: none -> 47.7 us  [exchange(): return lax.all_to_all(value, axes, 0, 0, tiled=False)]
    all_to_all x0 -> x3, waiting for transfers between devices: none -> 37.1 us  [exchange(): return lax.all_to_all(value, axes, 0, 0, tiled=False)]
    all_to_all x0 -> x3, starting transfers between devices: none -> 20.5 us  [exchange(): return lax.all_to_all(value, axes, 0, 0, tiled=False)]
  transfers between devices with their start and end apart: 2 -> 3, of which waited for: 2 -> 3; matrix products, arithmetic and copies ran while one was open for 0% -> 4% of each run, Pallas kernels for 0% -> 0%
where the time goes in v1:
time: 129 us
  blocking collectives  47.7 us (37%)
  waiting for transfers between devices  37.1 us (29%)
  starting transfers between devices  20.5 us (16%)
  local copies, waits for them, and re-layouts  11 us (9%)
  other arithmetic  6.73 us (5%)
  matrix products  4.05 us (3%)
  between operations  1.7 us (1%)
    all_to_all x1, blocking collectives, exchange(): return lax.all_to_all(value, axes, 0, 0, tiled=False)  47.7 us
    all_to_all x3, waiting for transfers between devices, exchange(): return lax.all_to_all(value, axes, 0, 0, tiled=False)  37.1 us
    all_to_all x3, starting transfers between devices, exchange(): return lax.all_to_all(value, axes, 0, 0, tiled=False)  20.5 us
  transfers between devices with their start and end apart: 3, of which 3 were waited for; matrix products, arithmetic and copies ran while one was open for 4% of the time, Pallas kernels for 0%

profile of v1, /device:TPU:1, one launch (start us, length us, event | category | flops | bytes accessed | tf_op | source)
XLA Modules:
  0.0 128.8 jit_solution(10492281278318321781)
XLA Ops:
  0.7 1.6 %slice.24 = bf16[4,198,512]{2,0,1:T(4,128)(2,1)S(1)} slice(bf16[4,199,512]{2,0,1:T(4,128)(2,1)} %param.9), slice={[0:4], [0:198], [0:512]} | slice | bytes 1622016 | tf_op jit(solution)/shard_map/slice | solution.py:19
  2.3 0.8 fusion.39
  3.1 0.3 multiply_reduce_fusion.2
  3.4 2.2 %multiply_reduce_fusion.1 = (f32[4,512]{1,0:T(4,128)S(1)}, f32[4,99,512]{2,1,0:T(8,128)S(1)}) fusion(f32[4,99,512]{2,1,0:T(8,128)S(1)} %get-tuple-element.19, f32[512]{0:T(512)S(1)} %copy-done.5, f32[512]{0:T(512)S(1)} %copy-done.6, f32[4,99]{1,0:T(4,128)S(1)} %fusion.32, f32[4,99]{1,0:T(4,128)S(1)} %broadcast_multiply_fusion.2), kind=kLoop, calls=%fused_computation.20 | loop fusion | flops 13987840 | bytes 1637472 | tf_op jit(solution)/shard_map/reduce_sum | solution.py:23
  5.7 0.5 broadcast_multiply_fusion
  6.2 0.7 multiply_reduce_fusion
  7.0 0.8 fusion.37
  7.8 0.3 copy-done.4
  8.1 0.9 bitcast_convert_fusion
  9.0 1.5 %copy.148 = bf16[2,16,32,512]{3,1,0,2:T(8,128)(2,1)} copy(bf16[2,16,32,512]{3,2,1,0:T(8,128)(2,1)S(1)} %bitcast.76) | data formatting | bytes 2097152 | tf_op jit(solution)/shard_map/reshape | solution.py:59
  10.6 10.6 %all-to-all-start = ((bf16[32,16,2,512]{3,1,2,0:T(8,128)(2,1)}), bf16[32,16,2,512]{3,1,2,0:T(8,128)(2,1)S(1)}, u32[]{:S(2)}, u32[]{:S(2)}) async-start(bf16[32,16,2,512]{3,1,2,0:T(8,128)(2,1)} %bitcast.71), calls=%async_computation | async-start | bytes 2097152 | tf_op jit(solution)/shard_map/all_to_all | solution.py:44
  21.2 16.9 %all-to-all-done = bf16[32,16,2,512]{3,1,2,0:T(8,128)(2,1)S(1)} async-done(((bf16[32,16,2,512]{3,1,2,0:T(8,128)(2,1)}), bf16[32,16,2,512]{3,1,2,0:T(8,128)(2,1)S(1)}, u32[]{:S(2)}, u32[]{:S(2)}) %all-to-all-start) | async-done | bytes 1048608 | tf_op jit(solution)/shard_map/all_to_all | solution.py:44
  38.1 0.2 reduce_sum.97
  38.4 0.3 broadcast_in_dim.13
  38.7 47.7 %all_to_all.20 = bf16[16,20,2,512]{3,2,1,0:T(2,128)(2,1)S(1)} all-to-all(bf16[16,20,2,512]{3,2,1,0:T(2,128)(2,1)S(1)} %broadcast_in_dim.13), channel_id=1, replica_groups=mesh['z'=16,'x'=4,'y'=4,'core'=2] {'z'}, dimensions={0} | all-to-all | bytes 1310720 | tf_op jit(solution)/shard_map/all_to_all | solution.py:44
  86.5 0.4 convert_reduce_fusion
  86.9 0.7 multiply_reduce_fusion.3
  87.6 1.3 %broadcast_in_dim_broadcast_in_dim_broadcast_in_dim.3 = f32[32,8,128]{2,1,0:T(8,128)} broadcast(f32[]{:T(128)} %multiply_reduce_fusion.3), dimensions={} | broadcast | bytes 131076 | tf_op jit(solution)/shard_map/broadcast_in_dim;broadcast_in_dim;broadcast_in_dim | solution.py:48
  88.9 5.8 %all-to-all-start.2 = ((f32[32,8,128]{2,1,0:T(8,128)}), f32[32,8,128]{2,1,0:T(8,128)S(1)}, u32[]{:S(2)}, u32[]{:S(2)}) async-start(f32[32,8,128]{2,1,0:T(8,128)} %broadcast_in_dim_broadcast_in_dim_broadcast_in_dim.3), calls=%async_computation.2 | async-start | bytes 262144 | tf_op jit(solution)/shard_map/all_to_all | solution.py:44
  94.7 0.1 slice.34
  94.9 7.6 %all-to-all-done.2 = f32[32,8,128]{2,1,0:T(8,128)S(1)} async-done(((f32[32,8,128]{2,1,0:T(8,128)}), f32[32,8,128]{2,1,0:T(8,128)S(1)}, u32[]{:S(2)}, u32[]{:S(2)}) %all-to-all-start.2) | async-done | bytes 131104 | tf_op jit(solution)/shard_map/all_to_all | solution.py:44
  102.5 0.6 slice_reduce_fusion
  103.8 0.1 subtract_convert_fusion
  103.9 1.1 broadcast_in_dim.14
  105.0 4.1 %all-to-all-start.3 = ((bf16[32,16,2,512]{3,1,2,0:T(8,128)(2,1)}), bf16[32,16,2,512]{3,1,2,0:T(8,128)(2,1)S(1)}, u32[]{:S(2)}, u32[]{:S(2)}) async-start(bf16[32,16,2,512]{3,1,2,0:T(8,128)(2,1)} %broadcast_in_dim.14), calls=%async_computation.3 | async-start | bytes 2097152 | tf_op jit(solution)/shard_map/all_to_all | solution.py:44
  109.1 1.9 %convolution_convert_fusion = bf16[4,99,2,512]{3,1,2,0:T(8,128)(2,1)S(1)} fusion(bf16[1,2,512,512]{3,1,2,0:T(2,128)(2,1)} %bitcast.79, f32[4,99,512]{2,1,0:T(8,128)S(1)} %copy-done.2, f32[4,99]{1,0:T(4,128)S(1)} %negate_multiply_fusion.1), kind=kOutput, calls=%fused_computation.1 | convolution fusion | flops 416047104 | bytes 2672176 | tf_op jit(solution)/shard_map/bfo,koi->bfki/dot_general | solution.py:31
  111.0 0.6 copy.106
  111.7 1.2 concatenate.6
  112.9 0.6 multiply_subtract_fusion
  113.5 12.6 %all-to-all-done.3 = bf16[32,16,2,512]{3,1,2,0:T(8,128)(2,1)S(1)} async-done(((bf16[32,16,2,512]{3,1,2,0:T(8,128)(2,1)}), bf16[32,16,2,512]{3,1,2,0:T(8,128)(2,1)S(1)}, u32[]{:S(2)}, u32[]{:S(2)}) %all-to-all-start.3) | async-done | bytes 1048608 | tf_op jit(solution)/shard_map/all_to_all | solution.py:44
  126.1 0.6 copy.118
  126.7 2.0 %copy.126 = bf16[1,2,512,512]{3,1,2,0:T(2,128)(2,1)} copy(bf16[1,2,512,512]{3,2,1,0:T(8,128)(2,1)S(1)} %bitcast.73) | data formatting | bytes 2097152
  (37 shorter events, 0.3 us)
Async XLA Ops:
  0.6 5.0 %copy-start = (bf16[512,1024]{1,0:T(8,128)(2,1)S(1)}, bf16[512,1024]{1,0:T(8,128)(2,1)}, u32[]{:S(2)}) copy-start(bf16[512,1024]{1,0:T(8,128)(2,1)} %param.13) | copy-start | bytes 3145732
  0.6 1.6 %copy-start.11 = (bf16[2,262144]{1,0:T(2,128)(2,1)S(1)}, bf16[2,262144]{1,0:T(2,128)(2,1)}, u32[]{:S(2)}) copy-start(bf16[2,262144]{1,0:T(2,128)(2,1)} %param.10) | copy-start | bytes 3145732
  2.2 0.9 copy-start.3
  2.3 1.2 copy-start.5
  2.3 1.2 copy-start.6
  3.4 2.3 %copy-start.7 = (f32[4,1024]{1,0:T(4,128)S(1)}, f32[4,1024]{1,0:T(4,128)}, u32[]{:S(2)}) copy-start(f32[4,1024]{1,0:T(4,128)} %param.14) | copy-start | bytes 49156
  6.9 1.2 copy-start.4
  7.8 1.2 copy-start.1
  10.6 10.6 %copy-start.8 = (f32[2,512]{1,0:T(2,128)S(1)}, f32[2,512]{1,0:T(2,128)}, u32[]{:S(2)}) copy-start(f32[2,512]{1,0:T(2,128)} %param.15) | copy-start | bytes 12292
  10.6 10.6 %copy-start.9 = (f32[2,512]{1,0:T(2,128)S(1)}, f32[2,512]{1,0:T(2,128)}, u32[]{:S(2)}) copy-start(f32[2,512]{1,0:T(2,128)} %param.16) | copy-start | bytes 12292
  10.6 10.7 %copy-start.10 = (f32[2,512]{1,0:T(2,128)S(1)}, f32[2,512]{1,0:T(2,128)}, u32[]{:S(2)}) copy-start(f32[2,512]{1,0:T(2,128)} %param.17) | copy-start | bytes 12292
  10.6 27.6 %all-to-all-start = ((bf16[32,16,2,512]{3,1,2,0:T(8,128)(2,1)}), bf16[32,16,2,512]{3,1,2,0:T(8,128)(2,1)S(1)}, u32[]{:S(2)}, u32[]{:S(2)}) async-start(bf16[32,16,2,512]{3,1,2,0:T(8,128)(2,1)} %bitcast.71), calls=%async_computation | async-start | bytes 2097152 | tf_op jit(solution)/shard_map/all_to_all | solution.py:44
  88.9 13.6 %all-to-all-start.2 = ((f32[32,8,128]{2,1,0:T(8,128)}), f32[32,8,128]{2,1,0:T(8,128)S(1)}, u32[]{:S(2)}, u32[]{:S(2)}) async-start(f32[32,8,128]{2,1,0:T(8,128)} %broadcast_in_dim_broadcast_in_dim_broadcast_in_dim.3), calls=%async_computation.2 | async-start | bytes 262144 | tf_op jit(solution)/shard_map/all_to_all | solution.py:44
  105.0 4.1 %copy-start.2 = (f32[4,99,512]{2,1,0:T(8,128)S(1)}, f32[4,99,512]{2,1,0:T(8,128)}, u32[]{:S(2)}) copy-start(f32[4,99,512]{2,1,0:T(8,128)} %copy-done.1) | copy-start | bytes 2433028
  105.0 21.1 %all-to-all-start.3 = ((bf16[32,16,2,512]{3,1,2,0:T(8,128)(2,1)}), bf16[32,16,2,512]{3,1,2,0:T(8,128)(2,1)S(1)}, u32[]{:S(2)}, u32[]{:S(2)}) async-start(bf16[32,16,2,512]{3,1,2,0:T(8,128)(2,1)} %broadcast_in_dim.14), calls=%async_computation.3 | async-start | bytes 2097152 | tf_op jit(solution)/shard_map/all_to_all | solution.py:44

commit v2 on v1

--- a/solution.py
+++ b/solution.py
@@ -62,7 +62,7 @@
     low = (master - high.astype(f32)).astype(bf16)
     state = jnp.stack([high, low, first_moment.astype(bf16), second_moment.astype(bf16)])
     packed = jnp.concatenate([part, state], axis=0)
-    column = spread(packed, "z", depth)
+    column = lax.all_gather(packed, "z")
     grad = jnp.sum(column[:, :depth].astype(f32), axis=0)
     state = column[:, depth:].astype(f32)
     piece = jnp.full((8, 128), jnp.sum(grad * grad), f32)

time: 129 us -> 117 us (0.907)
  blocking collectives: 47.7 us -> 30.1 us
  starting transfers between devices: 20.5 us -> 25.9 us
    all_to_all x1 -> x0, blocking collectives: 47.7 us -> none  [exchange(): return lax.all_to_all(value, axes, 0, 0, tiled=False)]
    all_gather x0 -> x1, blocking collectives: none -> 30.1 us  [body(): column = lax.all_gather(packed, 'z')]
    all_to_all x3, starting transfers between devices: 20.5 us -> 25.9 us  [exchange(): return lax.all_to_all(value, axes, 0, 0, tiled=False)]
where the time goes in v2:
time: 117 us; the launch traced here: 116 us
  waiting for transfers between devices  37.1 us (32%)
  blocking collectives  30.1 us (26%)
  starting transfers between devices  25.9 us (22%)
  local copies, waits for them, and re-layouts  10.6 us (9%)
  other arithmetic  6.73 us (6%)
  matrix products  4.05 us (3%)
  between operations  1.68 us (1%)
    all_to_all x3, waiting for transfers between devices, exchange(): return lax.all_to_all(value, axes, 0, 0, tiled=False)  37.1 us
    all_gather x1, blocking collectives, body(): column = lax.all_gather(packed, 'z')  30.1 us
    all_to_all x3, starting transfers between devices, exchange(): return lax.all_to_all(value, axes, 0, 0, tiled=False)  25.9 us
    unnamed x25, local copies, waits for them, and re-layouts  2.49 us
  transfers between devices with their start and end apart: 3, of which 3 were waited for; matrix products, arithmetic and copies ran while one was open for 4% of the time, Pallas kernels for 0%

profile of v2, /device:TPU:1, one launch (start us, length us, event | category | flops | bytes accessed | tf_op | source)
XLA Modules:
  0.0 116.3 jit_solution(15770256295926879893)
XLA Ops:
  0.7 1.6 %slice.24 = bf16[4,198,512]{2,0,1:T(4,128)(2,1)S(1)} slice(bf16[4,199,512]{2,0,1:T(4,128)(2,1)} %param.9), slice={[0:4], [0:198], [0:512]} | slice | bytes 1622016 | tf_op jit(solution)/shard_map/slice | solution.py:19
  2.3 0.8 fusion.39
  3.0 0.1 copy-done.3
  3.1 0.3 multiply_reduce_fusion.2
  3.4 2.2 %multiply_reduce_fusion.1 = (f32[4,512]{1,0:T(4,128)S(1)}, f32[4,99,512]{2,1,0:T(8,128)S(1)}) fusion(f32[4,99,512]{2,1,0:T(8,128)S(1)} %get-tuple-element.19, f32[512]{0:T(512)S(1)} %copy-done.5, f32[512]{0:T(512)S(1)} %copy-done.6, f32[4,99]{1,0:T(4,128)S(1)} %fusion.32, f32[4,99]{1,0:T(4,128)S(1)} %broadcast_multiply_fusion.2), kind=kLoop, calls=%fused_computation.20 | loop fusion | flops 13987840 | bytes 1637472 | tf_op jit(solution)/shard_map/reduce_sum | solution.py:23
  5.7 0.5 broadcast_multiply_fusion
  6.2 0.7 multiply_reduce_fusion
  7.0 0.8 fusion.37
  7.8 0.3 copy-done.4
  8.1 0.9 bitcast_convert_fusion
  9.0 1.5 %copy.151 = bf16[2,16,32,512]{3,1,0,2:T(8,128)(2,1)} copy(bf16[2,16,32,512]{3,2,1,0:T(8,128)(2,1)S(1)} %bitcast.79) | data formatting | bytes 2097152 | tf_op jit(solution)/shard_map/reshape | solution.py:59
  10.6 10.6 %all-to-all-start = ((bf16[32,16,2,512]{3,1,2,0:T(8,128)(2,1)}), bf16[32,16,2,512]{3,1,2,0:T(8,128)(2,1)S(1)}, u32[]{:S(2)}, u32[]{:S(2)}) async-start(bf16[32,16,2,512]{3,1,2,0:T(8,128)(2,1)} %bitcast.72), calls=%async_computation | async-start | bytes 2097152 | tf_op jit(solution)/shard_map/all_to_all | solution.py:44
  21.2 16.9 %all-to-all-done = bf16[32,16,2,512]{3,1,2,0:T(8,128)(2,1)S(1)} async-done(((bf16[32,16,2,512]{3,1,2,0:T(8,128)(2,1)}), bf16[32,16,2,512]{3,1,2,0:T(8,128)(2,1)S(1)}, u32[]{:S(2)}, u32[]{:S(2)}) %all-to-all-start) | async-done | bytes 1048608 | tf_op jit(solution)/shard_map/all_to_all | solution.py:44
  38.1 0.2 reduce_sum.97
  38.4 30.1 %all-gather = bf16[320,2,512]{2,1,0:T(2,128)(2,1)S(1)} all-gather(bf16[20,2,512]{2,1,0:T(2,128)(2,1)S(1)} %copy.117), channel_id=2, replica_groups=mesh['z'=16,'x'=4,'y'=4,'core'=2] {'z'}, dimensions={0}, use_global_device_ids=true | all-gather | bytes 696320 | tf_op jit(solution)/shard_map/all_gather | solution.py:65
  68.5 0.1 slice.34
  68.6 0.4 convert_reduce_fusion
  69.1 0.7 multiply_reduce_fusion.3
  69.7 1.3 %broadcast_in_dim_broadcast_in_dim_broadcast_in_dim.3 = f32[32,8,128]{2,1,0:T(8,128)} broadcast(f32[]{:T(128)} %multiply_reduce_fusion.3), dimensions={} | broadcast | bytes 131076 | tf_op jit(solution)/shard_map/broadcast_in_dim;broadcast_in_dim;broadcast_in_dim | solution.py:48
  71.0 11.3 %all-to-all-start.1 = ((f32[32,8,128]{2,1,0:T(8,128)}), f32[32,8,128]{2,1,0:T(8,128)S(1)}, u32[]{:S(2)}, u32[]{:S(2)}) async-start(f32[32,8,128]{2,1,0:T(8,128)} %broadcast_in_dim_broadcast_in_dim_broadcast_in_dim.3), calls=%async_computation.1 | async-start | bytes 262144 | tf_op jit(solution)/shard_map/all_to_all | solution.py:44
  82.3 7.6 %all-to-all-done.1 = f32[32,8,128]{2,1,0:T(8,128)S(1)} async-done(((f32[32,8,128]{2,1,0:T(8,128)}), f32[32,8,128]{2,1,0:T(8,128)S(1)}, u32[]{:S(2)}, u32[]{:S(2)}) %all-to-all-start.1) | async-done | bytes 131104 | tf_op jit(solution)/shard_map/all_to_all | solution.py:44
  90.0 0.6 slice_reduce_fusion
  91.3 0.1 subtract_convert_fusion
  91.4 1.1 broadcast_in_dim.11
  92.5 4.1 %all-to-all-start.2 = ((bf16[32,16,2,512]{3,1,2,0:T(8,128)(2,1)}), bf16[32,16,2,512]{3,1,2,0:T(8,128)(2,1)S(1)}, u32[]{:S(2)}, u32[]{:S(2)}) async-start(bf16[32,16,2,512]{3,1,2,0:T(8,128)(2,1)} %broadcast_in_dim.11), calls=%async_computation.2 | async-start | bytes 2097152 | tf_op jit(solution)/shard_map/all_to_all | solution.py:44
  96.6 1.9 %convolution_convert_fusion = bf16[4,99,2,512]{3,1,2,0:T(8,128)(2,1)S(1)} fusion(bf16[1,2,512,512]{3,1,2,0:T(2,128)(2,1)} %bitcast.82, f32[4,99,512]{2,1,0:T(8,128)S(1)} %copy-done.2, f32[4,99]{1,0:T(4,128)S(1)} %negate_multiply_fusion.1), kind=kOutput, calls=%fused_computation.1 | convolution fusion | flops 416047104 | bytes 2672176 | tf_op jit(solution)/shard_map/bfo,koi->bfki/dot_general | solution.py:31
  98.5 0.6 copy.109
  99.2 1.2 %concatenate.6 = bf16[4,199,512]{2,0,1:T(4,128)(2,1)} pad(bf16[4,198,512]{2,0,1:T(4,128)(2,1)S(1)} %bitcast.75, bf16[]{:T(256)} %constant.41.clone.1), padding=0_0x0_1x0_0 | pad | bytes 1626114 | tf_op jit(solution)/shard_map/concatenate | solution.py:36
  100.4 0.6 multiply_subtract_fusion
  101.0 12.6 %all-to-all-done.2 = bf16[32,16,2,512]{3,1,2,0:T(8,128)(2,1)S(1)} async-done(((bf16[32,16,2,512]{3,1,2,0:T(8,128)(2,1)}), bf16[32,16,2,512]{3,1,2,0:T(8,128)(2,1)S(1)}, u32[]{:S(2)}, u32[]{:S(2)}) %all-to-all-start.2) | async-done | bytes 1048608 | tf_op jit(solution)/shard_map/all_to_all | solution.py:44
  113.6 0.6 copy.121
  114.2 2.0 %copy.129 = bf16[1,2,512,512]{3,1,2,0:T(2,128)(2,1)} copy(bf16[1,2,512,512]{3,2,1,0:T(8,128)(2,1)S(1)} %bitcast.74) | data formatting | bytes 2097152
  (36 shorter events, 0.2 us)
Async XLA Ops:
  0.6 5.0 %copy-start = (bf16[512,1024]{1,0:T(8,128)(2,1)S(1)}, bf16[512,1024]{1,0:T(8,128)(2,1)}, u32[]{:S(2)}) copy-start(bf16[512,1024]{1,0:T(8,128)(2,1)} %param.13) | copy-start | bytes 3145732
  0.6 1.6 %copy-start.11 = (bf16[2,262144]{1,0:T(2,128)(2,1)S(1)}, bf16[2,262144]{1,0:T(2,128)(2,1)}, u32[]{:S(2)}) copy-start(bf16[2,262144]{1,0:T(2,128)(2,1)} %param.10) | copy-start | bytes 3145732
  2.2 0.9 copy-start.3
  2.3 1.2 copy-start.5
  2.3 1.2 copy-start.6
  3.4 2.3 %copy-start.7 = (f32[4,1024]{1,0:T(4,128)S(1)}, f32[4,1024]{1,0:T(4,128)}, u32[]{:S(2)}) copy-start(f32[4,1024]{1,0:T(4,128)} %param.14) | copy-start | bytes 49156
  6.9 1.2 copy-start.4
  7.8 1.2 %copy-start.1 = (f32[4,99,512]{2,1,0:T(8,128)}, f32[4,99,512]{2,1,0:T(8,128)S(1)}, u32[]{:S(2)}) copy-start(f32[4,99,512]{2,1,0:T(8,128)S(1)} %get-tuple-element.11) | copy-start | bytes 2433028
  10.6 10.6 %copy-start.8 = (f32[2,512]{1,0:T(2,128)S(1)}, f32[2,512]{1,0:T(2,128)}, u32[]{:S(2)}) copy-start(f32[2,512]{1,0:T(2,128)} %param.15) | copy-start | bytes 12292
  10.6 10.6 %copy-start.9 = (f32[2,512]{1,0:T(2,128)S(1)}, f32[2,512]{1,0:T(2,128)}, u32[]{:S(2)}) copy-start(f32[2,512]{1,0:T(2,128)} %param.16) | copy-start | bytes 12292
  10.6 10.7 %copy-start.10 = (f32[2,512]{1,0:T(2,128)S(1)}, f32[2,512]{1,0:T(2,128)}, u32[]{:S(2)}) copy-start(f32[2,512]{1,0:T(2,128)} %param.17) | copy-start | bytes 12292
  10.6 27.6 %all-to-all-start = ((bf16[32,16,2,512]{3,1,2,0:T(8,128)(2,1)}), bf16[32,16,2,512]{3,1,2,0:T(8,128)(2,1)S(1)}, u32[]{:S(2)}, u32[]{:S(2)}) async-start(bf16[32,16,2,512]{3,1,2,0:T(8,128)(2,1)} %bitcast.72), calls=%async_computation | async-start | bytes 2097152 | tf_op jit(solution)/shard_map/all_to_all | solution.py:44
  71.0 18.9 %all-to-all-start.1 = ((f32[32,8,128]{2,1,0:T(8,128)}), f32[32,8,128]{2,1,0:T(8,128)S(1)}, u32[]{:S(2)}, u32[]{:S(2)}) async-start(f32[32,8,128]{2,1,0:T(8,128)} %broadcast_in_dim_broadcast_in_dim_broadcast_in_dim.3), calls=%async_computation.1 | async-start | bytes 262144 | tf_op jit(solution)/shard_map/all_to_all | solution.py:44
  92.5 4.1 %copy-start.2 = (f32[4,99,512]{2,1,0:T(8,128)S(1)}, f32[4,99,512]{2,1,0:T(8,128)}, u32[]{:S(2)}) copy-start(f32[4,99,512]{2,1,0:T(8,128)} %copy-done.1) | copy-start | bytes 2433028
  92.5 21.1 %all-to-all-start.2 = ((bf16[32,16,2,512]{3,1,2,0:T(8,128)(2,1)}), bf16[32,16,2,512]{3,1,2,0:T(8,128)(2,1)S(1)}, u32[]{:S(2)}, u32[]{:S(2)}) async-start(bf16[32,16,2,512]{3,1,2,0:T(8,128)(2,1)} %broadcast_in_dim.11), calls=%async_computation.2 | async-start | bytes 2097152 | tf_op jit(solution)/shard_map/all_to_all | solution.py:44

commit v3 on v2

--- a/solution.py
+++ b/solution.py
@@ -1,6 +1,8 @@
 import jax
 import jax.numpy as jnp
 from jax import lax
+from jax.experimental import pallas as pl
+from jax.experimental.pallas import tpu as pltpu
 from jax.sharding import Mesh
 from jax.sharding import PartitionSpec as P
 
@@ -38,14 +40,72 @@
 
 AXES = ("z", "x", "y", "core")
 PLANE = ("x", "y", "core")
+LANES = 128
+
+
+def plane_sum(recv, master, first, second, out, rows):
+    taps, width = master.shape
+    depth = recv.shape[1]
+    total = recv[0].astype(jnp.float32)
+    for src in range(1, recv.shape[0]):
+        total += recv[src].astype(jnp.float32)
+    out[0:depth, :] = total.astype(jnp.bfloat16)
+    rows[...] = jnp.zeros_like(rows)
+    high = master[...].astype(jnp.bfloat16).astype(jnp.float32)
+    for row, value in enumerate((high, master[...] - high, first[...], second[...])):
+        for tap in range(taps):
+            rows[row : row + 1, tap * width : (tap + 1) * width] = value[tap : tap + 1, :]
+    out[depth:, :] = rows[...].astype(jnp.bfloat16)
+
+
+def column_sum(column, grad, piece):
+    depth = column.shape[0]
+    total = column[0, 0:depth, :].astype(jnp.float32)
+    for src in range(1, depth):
+        total += column[src, 0:depth, :].astype(jnp.float32)
+    grad[...] = total
+    squares = jnp.sum(jnp.sum(total * total, axis=0, keepdims=True), axis=1, keepdims=True)
+    piece[...] = jnp.broadcast_to(squares[None], piece.shape)
+
+
+def advance(scale, grad, master, first_moment, second_moment):
+    clipped = scale * grad
+    new_first = 0.9 * first_moment + 0.1 * clipped
+    new_second = 0.999 * second_moment + 0.001 * clipped * clipped
+    update = new_first / (1.0 - 0.9**20) / (jnp.sqrt(new_second / (1.0 - 0.999**20)) + 1e-08)
+    new_master = master - 0.0001 * (update + 0.01 * master)
+    return update, new_master, new_first, new_second
+
+
+def plane_update(pieces, grad, column, out, scale_out, state, rows, block, sems):
+    depth, taps = grad.shape[0], 2
+    squares = jnp.sum(pieces[...], axis=0)[0:1, 0:1]
+    scale = jnp.minimum(1.0, 1.0 / (jnp.sqrt(squares) + 1e-06))
+    scale_out[...] = jnp.broadcast_to(scale, scale_out.shape)
+    state[...] = column[:, depth:, :].astype(jnp.float32)
+    master = state[:, 0, :] + state[:, 1, :]
+    new_master = advance(scale, grad[...], master, state[:, 2, :], state[:, 3, :])[1]
+    parts = grad.shape[1] // LANES // taps
+    for tap in range(taps):
+        for part in range(parts):
+            start = (tap * parts + part) * LANES
+            rows[:, part * taps + tap, :] = new_master[:, start : start + LANES]
+    block[...] = rows[...].astype(jnp.bfloat16)
+    copies = [
+        pltpu.make_async_copy(block, out.at[peer], sems.at[peer]) for peer in range(out.shape[0])
+    ]
+    for copy in copies:
+        copy.start()
+    for copy in copies:
+        copy.wait()
+
+
+VMEM = pl.BlockSpec(memory_space=pltpu.VMEM)
+ANY = pl.BlockSpec(memory_space=pl.ANY)
 
 
 def exchange(value, axes):
     return lax.all_to_all(value, axes, 0, 0, tiled=False)
-
-
-def spread(value, axes, count):
-    return exchange(jnp.broadcast_to(value[None], (count,) + value.shape), axes)
 
 
 def body(
@@ -54,34 +114,47 @@
     depth, plane = lax.axis_size("z"), lax.axis_size(PLANE)
     taps, width = weights.shape[0], ln_gain.shape[0]
     f32, bf16 = jnp.float32, jnp.bfloat16
+    shape = jax.ShapeDtypeStruct
+    row = taps * width
     windows, dpre, input_grad = local_pass(inputs, weights, ln_gain, ln_bias, projection, targets)
-    term = jnp.einsum("bfo,bfki->koi", dpre, windows, preferred_element_type=f32).astype(bf16)
-    term = term.reshape(taps, depth, plane, width).transpose(2, 1, 0, 3)
-    part = jnp.sum(exchange(term, PLANE).astype(f32), axis=0).astype(bf16)
-    high = master.astype(bf16)
-    low = (master - high.astype(f32)).astype(bf16)
-    state = jnp.stack([high, low, first_moment.astype(bf16), second_moment.astype(bf16)])
-    packed = jnp.concatenate([part, state], axis=0)
+    term = jnp.einsum("bfo,bfki->oki", dpre, windows, preferred_element_type=f32).astype(bf16)
+    term = term.reshape(depth, plane, row).transpose(1, 0, 2)
+    packed = pl.pallas_call(
+        plane_sum,
+        out_shape=shape((depth + 8, row), bf16),
+        in_specs=[VMEM] * 4,
+        out_specs=VMEM,
+        scratch_shapes=[pltpu.VMEM((8, row), f32)],
+        name="plane_sum",
+    )(exchange(term, PLANE), master, first_moment, second_moment)
     column = lax.all_gather(packed, "z")
-    grad = jnp.sum(column[:, :depth].astype(f32), axis=0)
-    state = column[:, depth:].astype(f32)
-    piece = jnp.full((8, 128), jnp.sum(grad * grad), f32)
-    squares = jnp.sum(spread(piece, PLANE, plane)[:, 0, 0])
-    scale = jnp.minimum(1.0, 1.0 / (jnp.sqrt(squares) + 1e-06))
-
-    def advance(grad, master, first_moment, second_moment):
-        clipped = scale * grad
-        new_first = 0.9 * first_moment + 0.1 * clipped
-        new_second = 0.999 * second_moment + 0.001 * clipped * clipped
-        update = new_first / (1.0 - 0.9**20) / (jnp.sqrt(new_second / (1.0 - 0.999**20)) + 1e-08)
-        new_master = master - 0.0001 * (update + 0.01 * master)
-        return update, new_master, new_first, new_second
-
-    mine = lax.dynamic_index_in_dim(grad, lax.axis_index("z"), 0, keepdims=False)
-    update, new_master, new_first, new_second = advance(mine, master, first_moment, second_moment)
-    rows = advance(grad, state[:, 0] + state[:, 1], state[:, 2], state[:, 3])[1].astype(bf16)
-    whole = spread(rows, PLANE, plane)
-    new_weights = whole.transpose(2, 1, 0, 3).reshape(taps, -1)
+    grad, piece = pl.pallas_call(
+        column_sum,
+        out_shape=(shape((depth, row), f32), shape((plane, 8, LANES), f32)),
+        in_specs=[VMEM],
+        out_specs=(VMEM, VMEM),
+        name="column_sum",
+    )(column)
+    rows, scale = pl.pallas_call(
+        plane_update,
+        out_shape=(shape((plane, depth, row // LANES, LANES), bf16), shape((8, LANES), f32)),
+        in_specs=[VMEM] * 3,
+        out_specs=(ANY, VMEM),
+        scratch_shapes=[
+            pltpu.VMEM((depth, 8, row), f32),
+            pltpu.VMEM((depth, row // LANES, LANES), f32),
+            pltpu.VMEM((depth, row // LANES, LANES), bf16),
+            pltpu.SemaphoreType.DMA((plane,)),
+        ],
+        name="plane_update",
+    )(exchange(piece, PLANE), grad, column)
+    mine = lax.dynamic_slice_in_dim(grad, lax.axis_index("z"), 1, 0).reshape(taps, width)
+    update, new_master, new_first, new_second = advance(
+        scale[0, 0], mine, master, first_moment, second_moment
+    )
+    whole = exchange(rows, PLANE).transpose(1, 0, 2, 3)
+    whole = whole.reshape(depth * plane * width // LANES, taps, LANES).transpose(1, 0, 2)
+    new_weights = whole.reshape(taps, -1)
     return (input_grad, update, new_master, new_first, new_second, new_weights)
 
 

time: 117 us -> 122 us (1.043)
  blocking collectives: 30.1 us -> 80 us
  waiting for transfers between devices: 37.1 us -> 9.93 us
  starting transfers between devices: 25.9 us -> 4.12 us
  Pallas kernels: 0 us -> 7.25 us
  local copies, waits for them, and re-layouts: 10.6 us -> 9.35 us
    all_to_all x0 -> x2, blocking collectives: none -> 46.3 us  [exchange(): return lax.all_to_all(value, axes, 0, 0, tiled=False)]
    all_to_all x3 -> x1, waiting for transfers between devices: 37.1 us -> 9.93 us  [exchange(): return lax.all_to_all(value, axes, 0, 0, tiled=False)]
    all_to_all x3 -> x1, starting transfers between devices: 25.9 us -> 4.12 us  [exchange(): return lax.all_to_all(value, axes, 0, 0, tiled=False)]
    pallas_call x0 -> x3, Pallas kernels: none -> 7.25 us  [the longest x1 3.28 us: body(): pl.pallas_call(plane_update, out_shape=(shape((plane, depth, row // LANES...]
    all_gather x1, blocking collectives: 30.1 us -> 33.7 us  [body(): column = lax.all_gather(packed, 'z')]
    reduce_sum x4 -> x0, other arithmetic: 1.9 us -> none  [the longest x1 0.67 us: body(): piece = jnp.full((8, 128), jnp.sum(grad * grad), f32)]
    mul x0 -> x1, other arithmetic: none -> 1.42 us  [advance(): clipped = scale * grad]
    unnamed x25 -> x24, local copies, waits for them, and re-layouts: 2.49 us -> 1.07 us
  transfers between devices with their start and end apart: 3 -> 1, of which waited for: 3 -> 1; matrix products, arithmetic and copies ran while one was open for 4% -> 6% of each run, Pallas kernels for 0% -> 0%
where the time goes in v3:
time: 122 us
  blocking collectives  80 us (66%)
  waiting for transfers between devices  9.93 us (8%)
  local copies, waits for them, and re-layouts  9.35 us (8%)
  Pallas kernels  7.25 us (6%)
  other arithmetic  6.11 us (5%)
  starting transfers between devices  4.12 us (3%)
  matrix products  4.05 us (3%)
    all_to_all x2, blocking collectives, exchange(): return lax.all_to_all(value, axes, 0, 0, tiled=False)  46.3 us
    all_gather x1, blocking collectives, body(): column = lax.all_gather(packed, 'z')  33.7 us
    all_to_all x1, waiting for transfers between devices, exchange(): return lax.all_to_all(value, axes, 0, 0, tiled=False)  9.93 us
    all_to_all x1, starting transfers between devices, exchange(): return lax.all_to_all(value, axes, 0, 0, tiled=False)  4.12 us
    pallas_call x1, Pallas kernels, body(): pl.pallas_call(plane_update, out_shape=(shape((plane, depth, row // LANES...  3.28 us
  transfers between devices with their start and end apart: 1, of which 1 were waited for; matrix products, arithmetic and copies ran while one was open for 6% of the time, Pallas kernels for 0%

profile of v3, /device:TPU:1, one launch (start us, length us, event | category | flops | bytes accessed | tf_op | source)
XLA Modules:
  0.0 121.7 jit_solution(2278252931381053301)
XLA Ops:
  0.6 0.0 copy-start
  0.7 1.6 %slice.6 = bf16[4,198,512]{2,0,1:T(4,128)(2,1)S(1)} slice(bf16[4,199,512]{2,0,1:T(4,128)(2,1)} %param.9), slice={[0:4], [0:198], [0:512]} | slice | bytes 1622016 | tf_op jit(solution)/shard_map/slice | solution.py:21
  2.3 0.0 copy-start.6
  2.3 0.8 fusion.25
  3.0 0.1 copy-done.3
  3.1 0.3 multiply_reduce_fusion.2
  3.4 0.0 copy-start.7
  3.4 2.2 %multiply_reduce_fusion.1 = (f32[4,512]{1,0:T(4,128)S(1)}, f32[4,99,512]{2,1,0:T(8,128)S(1)}) fusion(f32[4,99,512]{2,1,0:T(8,128)S(1)} %get-tuple-element.25, f32[512]{0:T(512)S(1)} %copy-done.5, f32[512]{0:T(512)S(1)} %copy-done.6, f32[4,99]{1,0:T(4,128)S(1)} %fusion.19, f32[4,99]{1,0:T(4,128)S(1)} %broadcast_multiply_fusion.2), kind=kLoop, calls=%fused_computation.19 | loop fusion | flops 13987840 | bytes 1637472 | tf_op jit(solution)/shard_map/reduce_sum | solution.py:25
  5.7 0.5 broadcast_multiply_fusion
  6.2 0.7 multiply_reduce_fusion
  6.9 0.0 copy-start.4
  7.0 0.8 fusion.23
  7.8 0.9 copy-done.1
  8.7 0.9 bitcast_convert_fusion
  9.6 1.1 copy.19
  10.7 0.8 reshape.64
  11.5 0.6 copy.43
  12.1 27.2 %all_to_all.15.recv = bf16[32,16,1024]{2,1,0:T(8,128)(2,1)} all-to-all(bf16[32,16,1024]{2,1,0:T(8,128)(2,1)S(1)} %bitcast.41), channel_id=1, replica_groups=mesh['z'=16,'x'=4,'y'=4,'core'=2] {'x','y','core'}, dimensions={0} | all-to-all | bytes 2097152 | tf_op jit(solution)/shard_map/all_to_all | solution.py:108
  39.2 2.0 %plane_sum.1 = bf16[24,1024]{1,0:T(8,128)(2,1)} custom-call(bf16[32,16,1024]{2,1,0:T(8,128)(2,1)} %all_to_all.15.recv, f32[2,512]{1,0:T(2,128)} %master.1, f32[2,512]{1,0:T(2,128)} %first.1, f32[2,512]{1,0:T(2,128)} %second.1), custom_call_target="tpu_custom_call" | custom-call | tf_op jit(solution)/shard_map/plane_sum/pallas_call | solution.py:122
  41.3 33.7 %all-gather = bf16[384,1024]{1,0:T(8,128)(2,1)} all-gather(bf16[24,1024]{1,0:T(8,128)(2,1)} %plane_sum.1), channel_id=2, replica_groups=mesh['z'=16,'x'=4,'y'=4,'core'=2] {'z'}, dimensions={0}, use_global_device_ids=true | all-gather | bytes 835584 | tf_op jit(solution)/shard_map/all_gather | solution.py:130
  74.9 2.0 %column_sum.1 = (f32[16,1024]{1,0:T(8,128)}, f32[32,8,128]{2,1,0:T(8,128)}) custom-call(bf16[16,24,1024]{2,1,0:T(8,128)(2,1)} %bitcast.38), custom_call_target="tpu_custom_call" | custom-call | tf_op jit(solution)/shard_map/column_sum/pallas_call | solution.py:131
  76.9 19.1 %all_to_all.16.pieces = f32[32,8,128]{2,1,0:T(8,128)} all-to-all(f32[32,8,128]{2,1,0:T(8,128)} %get-tuple-element.10), channel_id=1, replica_groups=mesh['z'=16,'x'=4,'y'=4,'core'=2] {'x','y','core'}, dimensions={0} | all-to-all | bytes 262144 | tf_op jit(solution)/shard_map/all_to_all | solution.py:108
  96.0 3.3 %plane_update.1 = (bf16[32,16,8,128]{3,2,1,0:T(8,128)(2,1)}, f32[8,128]{1,0:T(8,128)}) custom-call(f32[32,8,128]{2,1,0:T(8,128)} %all_to_all.16.pieces, f32[16,1024]{1,0:T(8,128)} %get-tuple-element.11.grad, bf16[16,24,1024]{2,1,0:T(8,128)(2,1)} %bitcast.39), custom_call_target="tpu_custom_call" | custom-call | tf_op jit(solution)/shard_map/plane_update/pallas_call | solution.py:138
  99.3 4.1 %all-to-all-start.2 = ((bf16[32,16,8,128]{3,2,1,0:T(8,128)(2,1)}), bf16[32,16,8,128]{3,2,1,0:T(8,128)(2,1)S(1)}, u32[]{:S(2)}, u32[]{:S(2)}) async-start(bf16[32,16,8,128]{3,2,1,0:T(8,128)(2,1)} %get-tuple-element.13), calls=%async_computation.2 | async-start | bytes 2097152 | tf_op jit(solution)/shard_map/all_to_all | solution.py:108
  103.5 1.9 %convolution_convert_fusion = bf16[4,99,2,512]{3,1,2,0:T(8,128)(2,1)S(1)} fusion(bf16[1,2,512,512]{3,1,2,0:T(2,128)(2,1)} %bitcast.46, f32[4,99,512]{2,1,0:T(8,128)S(1)} %copy-done.2, f32[4,99]{1,0:T(4,128)S(1)} %negate_multiply_fusion.1), kind=kOutput, calls=%fused_computation.1 | convolution fusion | flops 416047104 | bytes 2672176 | tf_op jit(solution)/shard_map/bfo,koi->bfki/dot_general | solution.py:33
  105.3 0.6 copy.17
  106.0 1.2 concatenate.3
  107.2 1.2 slice.7
  108.4 1.4 %multiply_reduce_fusion.3 = f32[1024]{0:T(1024)S(1)} fusion(f32[16,1024]{1,0:T(8,128)} %get-tuple-element.11.grad, s32[]{:T(128)S(6)} %select_n.3, f32[]{:T(128)} %bitcast.10), kind=kLoop, calls=%fused_computation.43 | loop fusion | flops 1024 | bytes 8200 | tf_op jit(solution)/shard_map/mul | solution.py:72
  109.9 0.6 multiply_subtract_fusion
  110.5 9.9 %all-to-all-done.2 = bf16[32,16,8,128]{3,2,1,0:T(8,128)(2,1)S(1)} async-done(((bf16[32,16,8,128]{3,2,1,0:T(8,128)(2,1)}), bf16[32,16,8,128]{3,2,1,0:T(8,128)(2,1)S(1)}, u32[]{:S(2)}, u32[]{:S(2)}) %all-to-all-start.2) | async-done | bytes 1048608 | tf_op jit(solution)/shard_map/all_to_all | solution.py:108
  120.5 1.2 %copy.21 = bf16[16,32,8,128]{3,2,1,0:T(8,128)(2,1)} copy(bf16[16,32,8,128]{3,2,0,1:T(8,128)(2,1)S(1)} %bitcast.40) | data formatting | bytes 2097152 | tf_op jit(solution)/shard_map/transpose | solution.py:155
  (23 shorter events, 0.1 us)
Async XLA Ops:
  0.6 5.0 %copy-start = (bf16[512,1024]{1,0:T(8,128)(2,1)S(1)}, bf16[512,1024]{1,0:T(8,128)(2,1)}, u32[]{:S(2)}) copy-start(bf16[512,1024]{1,0:T(8,128)(2,1)} %param.13) | copy-start | bytes 3145732
  0.6 1.6 %copy-start.11 = (bf16[2,262144]{1,0:T(2,128)(2,1)S(1)}, bf16[2,262144]{1,0:T(2,128)(2,1)}, u32[]{:S(2)}) copy-start(bf16[2,262144]{1,0:T(2,128)(2,1)} %param.10) | copy-start | bytes 3145732
  2.2 0.9 copy-start.3
  2.3 1.2 copy-start.5
  2.3 1.2 copy-start.6
  3.4 2.3 %copy-start.7 = (f32[4,1024]{1,0:T(4,128)S(1)}, f32[4,1024]{1,0:T(4,128)}, u32[]{:S(2)}) copy-start(f32[4,1024]{1,0:T(4,128)} %param.14) | copy-start | bytes 49156
  6.9 1.8 %copy-start.4 = (bf16[4,198,512]{2,0,1:T(4,128)(2,1)S(1)}, bf16[4,198,512]{2,0,1:T(4,128)(2,1)}, u32[]{:S(2)}) copy-start(bf16[4,198,512]{2,0,1:T(4,128)(2,1)} %copy-done.3) | copy-start | bytes 2433028
  7.8 0.9 copy-start.1
  99.3 4.1 %copy-start.2 = (f32[4,99,512]{2,1,0:T(8,128)S(1)}, f32[4,99,512]{2,1,0:T(8,128)}, u32[]{:S(2)}) copy-start(f32[4,99,512]{2,1,0:T(8,128)} %copy-done.1) | copy-start | bytes 2433028
  99.3 21.1 %all-to-all-start.2 = ((bf16[32,16,8,128]{3,2,1,0:T(8,128)(2,1)}), bf16[32,16,8,128]{3,2,1,0:T(8,128)(2,1)S(1)}, u32[]{:S(2)}, u32[]{:S(2)}) async-start(bf16[32,16,8,128]{3,2,1,0:T(8,128)(2,1)} %get-tuple-element.13), calls=%async_computation.2 | async-start | bytes 2097152 | tf_op jit(solution)/shard_map/all_to_all | solution.py:108
  106.0 3.9 %copy-start.8 = (f32[2,512]{1,0:T(2,128)S(1)}, f32[2,512]{1,0:T(2,128)}, u32[]{:S(2)}) copy-start(f32[2,512]{1,0:T(2,128)} %master.1) | copy-start | bytes 12292
  106.0 3.9 %copy-start.9 = (f32[2,512]{1,0:T(2,128)S(1)}, f32[2,512]{1,0:T(2,128)}, u32[]{:S(2)}) copy-start(f32[2,512]{1,0:T(2,128)} %first.1) | copy-start | bytes 12292
  106.0 3.9 %copy-start.10 = (f32[2,512]{1,0:T(2,128)S(1)}, f32[2,512]{1,0:T(2,128)}, u32[]{:S(2)}) copy-start(f32[2,512]{1,0:T(2,128)} %second.1) | copy-start | bytes 12292

commit v4 on v2

--- a/solution.py
+++ b/solution.py
@@ -1,6 +1,8 @@
 import jax
 import jax.numpy as jnp
 from jax import lax
+from jax.experimental import pallas as pl
+from jax.experimental.pallas import tpu as pltpu
 from jax.sharding import Mesh
 from jax.sharding import PartitionSpec as P
 
@@ -38,14 +40,91 @@
 
 AXES = ("z", "x", "y", "core")
 PLANE = ("x", "y", "core")
+LANES = 128
+LIMIT = 4 * 2**20
+
+
+def plane_sum(recv, out):
+    peers, taps, depth, width = recv.shape
+    parts = width // LANES
+    for tap in range(taps):
+        total = recv[0, tap].astype(jnp.float32)
+        for src in range(1, peers):
+            total += recv[src, tap].astype(jnp.float32)
+        for part in range(parts):
+            out[:, part * taps + tap, :] = total[:, part * LANES : (part + 1) * LANES]
+
+
+def column_pack(recv, master, first, second, grad, out):
+    total = jnp.sum(recv[...], axis=0)
+    grad[...] = total
+    high = master[...].astype(jnp.bfloat16)
+    low = (master[...] - high.astype(jnp.float32)).astype(jnp.bfloat16)
+    rows = (total.astype(jnp.bfloat16), high, low)
+    rows += (first[...].astype(jnp.bfloat16), second[...].astype(jnp.bfloat16))
+    for index, row in enumerate(rows):
+        for peer in range(out.shape[0]):
+            out[peer, index] = row
+
+
+def column_squares(column, piece):
+    grad = column[:, 0].astype(jnp.float32)
+    squares = jnp.sum(grad * grad, axis=0)
+    squares = jnp.sum(jnp.sum(squares, axis=0, keepdims=True), axis=1, keepdims=True)
+    piece[...] = jnp.broadcast_to(squares[None], piece.shape)
+
+
+def advance(scale, grad, master, first_moment, second_moment):
+    clipped = scale * grad
+    new_first = 0.9 * first_moment + 0.1 * clipped
+    new_second = 0.999 * second_moment + 0.001 * clipped * clipped
+    update = new_first / (1.0 - 0.9**20) / (jnp.sqrt(new_second / (1.0 - 0.999**20)) + 1e-08)
+    new_master = master - 0.0001 * (update + 0.01 * master)
+    return update, new_master, new_first, new_second
+
+
+def plane_update(pieces, column, out, scale_out, block, sems):
+    squares = jnp.sum(pieces[...], axis=0)[0:1, 0:1]
+    scale = jnp.minimum(1.0, 1.0 / (jnp.sqrt(squares) + 1e-06))
+    scale_out[...] = jnp.broadcast_to(scale, scale_out.shape)
+    grad, high, low, first, second = (column[:, i].astype(jnp.float32) for i in range(5))
+    block[...] = advance(scale[None], grad, high + low, first, second)[1].astype(jnp.bfloat16)
+    copies = [
+        pltpu.make_async_copy(block, out.at[peer], sems.at[peer]) for peer in range(out.shape[0])
+    ]
+    for copy in copies:
+        copy.start()
+    for copy in copies:
+        copy.wait()
+
+
+VMEM = pl.BlockSpec(memory_space=pltpu.VMEM)
+ANY = pl.BlockSpec(memory_space=pl.ANY)
+
+
+def local(kernel, out_shape, count, out_specs=VMEM, scratch=()):
+    return pl.pallas_call(
+        kernel,
+        out_shape=out_shape,
+        in_specs=[VMEM] * count,
+        out_specs=out_specs,
+        scratch_shapes=list(scratch),
+        compiler_params=pltpu.CompilerParams(vmem_limit_bytes=LIMIT),
+        name=kernel.__name__,
+    )
 
 
 def exchange(value, axes):
     return lax.all_to_all(value, axes, 0, 0, tiled=False)
 
 
-def spread(value, axes, count):
-    return exchange(jnp.broadcast_to(value[None], (count,) + value.shape), axes)
+def to_rows(shard):
+    taps = shard.shape[0]
+    return shard.reshape(taps, -1, LANES).transpose(1, 0, 2).reshape(-1, LANES)
+
+
+def from_rows(rows, taps):
+    return rows.reshape(-1, taps, LANES).transpose(1, 0, 2).reshape(taps, -1)
 
 
 def body(
@@ -53,35 +132,33 @@
 ):
     depth, plane = lax.axis_size("z"), lax.axis_size(PLANE)
     taps, width = weights.shape[0], ln_gain.shape[0]
+    tile = (taps * width // LANES, LANES)
     f32, bf16 = jnp.float32, jnp.bfloat16
+    shape = jax.ShapeDtypeStruct
     windows, dpre, input_grad = local_pass(inputs, weights, ln_gain, ln_bias, projection, targets)
-    term = jnp.einsum("bfo,bfki->koi", dpre, windows, preferred_element_type=f32).astype(bf16)
-    term = term.reshape(taps, depth, plane, width).transpose(2, 1, 0, 3)
-    part = jnp.sum(exchange(term, PLANE).astype(f32), axis=0).astype(bf16)
-    high = master.astype(bf16)
-    low = (master - high.astype(f32)).astype(bf16)
-    state = jnp.stack([high, low, first_moment.astype(bf16), second_moment.astype(bf16)])
-    packed = jnp.concatenate([part, state], axis=0)
-    column = lax.all_gather(packed, "z")
-    grad = jnp.sum(column[:, :depth].astype(f32), axis=0)
-    state = column[:, depth:].astype(f32)
-    piece = jnp.full((8, 128), jnp.sum(grad * grad), f32)
-    squares = jnp.sum(spread(piece, PLANE, plane)[:, 0, 0])
-    scale = jnp.minimum(1.0, 1.0 / (jnp.sqrt(squares) + 1e-06))
-
-    def advance(grad, master, first_moment, second_moment):
-        clipped = scale * grad
-        new_first = 0.9 * first_moment + 0.1 * clipped
-        new_second = 0.999 * second_moment + 0.001 * clipped * clipped
-        update = new_first / (1.0 - 0.9**20) / (jnp.sqrt(new_second / (1.0 - 0.999**20)) + 1e-08)
-        new_master = master - 0.0001 * (update + 0.01 * master)
-        return update, new_master, new_first, new_second
-
-    mine = lax.dynamic_index_in_dim(grad, lax.axis_index("z"), 0, keepdims=False)
-    update, new_master, new_first, new_second = advance(mine, master, first_moment, second_moment)
-    rows = advance(grad, state[:, 0] + state[:, 1], state[:, 2], state[:, 3])[1].astype(bf16)
-    whole = spread(rows, PLANE, plane)
-    new_weights = whole.transpose(2, 1, 0, 3).reshape(taps, -1)
+    order = jnp.arange(width).reshape(depth, plane).T.reshape(-1)
+    pick = (jnp.arange(width)[:, None] == order[None, :]).astype(bf16)
+    moved = jnp.einsum("bfo,op->bfp", dpre, pick, preferred_element_type=f32).astype(bf16)
+    term = jnp.einsum("bfo,bfki->koi", moved, windows, preferred_element_type=f32).astype(bf16)
+    term = term.reshape(taps, plane, depth, width).transpose(1, 0, 2, 3)
+    part = local(plane_sum, shape((depth,) + tile, f32), 1)(exchange(term, PLANE))
+    shards = [to_rows(value) for value in (master, first_moment, second_moment)]
+    grad, packed = local(
+        column_pack, (shape(tile, f32), shape((depth, 5) + tile, bf16)), 4, (VMEM, VMEM)
+    )(exchange(part, "z"), *shards)
+    column = exchange(packed, "z")
+    piece = local(column_squares, shape((plane, 8, LANES), f32), 1)(column)
+    rows, scale = local(
+        plane_update,
+        (shape((plane, depth) + tile, bf16), shape((8, LANES), f32)),
+        2,
+        (ANY, VMEM),
+        (pltpu.VMEM((depth,) + tile, bf16), pltpu.SemaphoreType.DMA((plane,))),
+    )(exchange(piece, PLANE), column)
+    fresh = [from_rows(value, taps) for value in advance(scale, grad, *shards)]
+    update, new_master, new_first, new_second = fresh
+    whole = exchange(rows, PLANE).transpose(1, 0, 2, 3)
+    new_weights = from_rows(whole, taps)
     return (input_grad, update, new_master, new_first, new_second, new_weights)
 
 

time: 117 us -> 119 us (1.017)
  blocking collectives: 30.1 us -> 82.9 us
  waiting for transfers between devices: 37.1 us -> 12.6 us
  starting transfers between devices: 25.9 us -> 4.12 us
  local copies, waits for them, and re-layouts: 10.6 us -> 4.93 us
  Pallas kernels: 0 us -> 1.69 us
  matrix products: 4.05 us -> 5.73 us
  other arithmetic: 6.73 us -> 5.53 us
    all_to_all x0 -> x4, blocking collectives: none -> 82.9 us  [exchange(): return lax.all_to_all(value, axes, 0, 0, tiled=False)]
    all_gather x1 -> x0, blocking collectives: 30.1 us -> none  [body(): column = lax.all_gather(packed, 'z')]
    all_to_all x3 -> x1, waiting for transfers between devices: 37.1 us -> 12.6 us  [exchange(): return lax.all_to_all(value, axes, 0, 0, tiled=False)]
    all_to_all x3 -> x1, starting transfers between devices: 25.9 us -> 4.12 us  [exchange(): return lax.all_to_all(value, axes, 0, 0, tiled=False)]
    unnamed x25 -> x20, local copies, waits for them, and re-layouts: 2.49 us -> 0.13 us
    reduce_sum x4 -> x0, other arithmetic: 1.9 us -> none  [the longest x1 0.67 us: body(): piece = jnp.full((8, 128), jnp.sum(grad * grad), f32)]
    pallas_call x0 -> x4, Pallas kernels: none -> 1.69 us  [the longest x1 1.37 us: body(): local(plane_update, (shape((plane, depth) + tile, bf16), shape((8, LANES)...]
    dot_general x1, matrix products: 0.9 us -> 2.58 us  [body(): jnp.einsum('bfo,bfki->koi', moved, windows, preferred_element_type=f32)]
  transfers between devices with their start and end apart: 3 -> 1, of which waited for: 3 -> 1; matrix products, arithmetic and copies ran while one was open for 4% -> 4% of each run, Pallas kernels for 0% -> 0%
where the time goes in v4:
time: 119 us; the launch traced here: 118 us
  blocking collectives  82.9 us (70%)
  waiting for transfers between devices  12.6 us (11%)
  matrix products  5.73 us (5%)
  other arithmetic  5.53 us (5%)
  local copies, waits for them, and re-layouts  4.93 us (4%)
  starting transfers between devices  4.12 us (3%)
  Pallas kernels  1.69 us (1%)
    all_to_all x4, blocking collectives, exchange(): return lax.all_to_all(value, axes, 0, 0, tiled=False)  82.9 us
    all_to_all x1, waiting for transfers between devices, exchange(): return lax.all_to_all(value, axes, 0, 0, tiled=False)  12.6 us
    all_to_all x1, starting transfers between devices, exchange(): return lax.all_to_all(value, axes, 0, 0, tiled=False)  4.12 us
    dot_general x1, matrix products, body(): jnp.einsum('bfo,bfki->koi', moved, windows, preferred_element_type=f32)  2.58 us
  transfers between devices with their start and end apart: 1, of which 1 were waited for; matrix products, arithmetic and copies ran while one was open for 4% of the time, Pallas kernels for 0%

profile of v4, /device:TPU:1, one launch (start us, length us, event | category | flops | bytes accessed | tf_op | source)
XLA Modules:
  0.0 118.4 jit_solution(3215929493073495253)
XLA Ops:
  0.6 0.0 copy-start
  0.6 0.0 copy-start.9
  0.7 1.6 %slice.3 = bf16[4,198,512]{2,0,1:T(4,128)(2,1)S(1)} slice(bf16[4,199,512]{2,0,1:T(4,128)(2,1)} %param.9), slice={[0:4], [0:198], [0:512]} | slice | bytes 1622016 | tf_op jit(solution)/shard_map/slice | solution.py:21
  2.2 0.0 copy-start.5
  2.3 0.0 copy-start.6
  2.3 0.0 copy-start.7
  2.3 0.8 fusion.31
  3.1 0.1 copy-done.5
  3.1 0.3 multiply_reduce_fusion.2
  3.4 0.0 copy-start.8
  3.4 0.0 copy-done.6
  3.4 2.2 %multiply_reduce_fusion.1 = (f32[4,512]{1,0:T(4,128)S(1)}, f32[4,99,512]{2,1,0:T(8,128)S(1)}) fusion(f32[4,99,512]{2,1,0:T(8,128)S(1)} %get-tuple-element.25, f32[512]{0:T(512)S(1)} %copy-done.6, f32[512]{0:T(512)S(1)} %copy-done.7, f32[4,99]{1,0:T(4,128)S(1)} %fusion.25, f32[4,99]{1,0:T(4,128)S(1)} %broadcast_multiply_fusion.2), kind=kLoop, calls=%fused_computation.23 | loop fusion | flops 13987840 | bytes 1637472 | tf_op jit(solution)/shard_map/reduce_sum | solution.py:25
  5.7 0.5 broadcast_multiply_fusion
  6.2 0.7 multiply_reduce_fusion
  7.0 1.7 %fusion.29 = (f32[4,99]{1,0:T(4,128)S(1)}, f32[4,99,512]{2,1,0:T(8,128)}) fusion(f32[4,99]{1,0:T(4,128)S(1)} %multiply_multiply_fusion.6, f32[4,99,512]{2,1,0:T(8,128)S(1)} %get-tuple-element.21, f32[4,512]{1,0:T(4,128)S(1)} %get-tuple-element.23, f32[4,512]{1,0:T(4,128)S(1)} %get-tuple-element.22, f32[512]{0:T(512)S(1)} %copy-done.6, f32[512]{0:T(512)S(1)} %copy-done.7, ...), kind=kLoop, calls=%fused_computation.57 | loop fusion | flops 4460148 | bytes 2459840 | tf_op jit(solution)/shard_map/transpose(jvp())/reduce_sum | solution.py:11
  8.6 0.1 reshape.134
  8.7 2.6 %bitcast_convert_fusion = bf16[512,2,512]{2,0,1:T(8,128)(2,1)S(1)} fusion(bf16[4,99,2,512]{3,0,2,1:T(4,128)(2,1)} %bitcast.93, s32[512]{0:T(512)S(1)} %reshape.134, f32[4,99,512]{2,1,0:T(8,128)} %get-tuple-element.19, f32[4,99]{1,0:T(4,128)S(1)} %negate_multiply_fusion.1), kind=kOutput, calls=%fused_computation | convolution fusion | flops 624248832 | bytes 2674224 | tf_op jit(solution)/shard_map/bfo,bfki->koi/dot_general | solution.py:142
  11.3 0.1 copy.56
  11.4 26.5 %all_to_all.25.recv = bf16[32,2,16,512]{3,2,1,0:T(8,128)(2,1)S(1)} all-to-all(bf16[32,2,16,512]{3,2,1,0:T(8,128)(2,1)S(1)} %bitcast.88), channel_id=1, replica_groups=mesh['z'=16,'x'=4,'y'=4,'core'=2] {'x','y','core'}, dimensions={0} | all-to-all | bytes 2097152 | tf_op jit(solution)/shard_map/all_to_all | solution.py:118
  37.9 0.2 plane_sum.1
  38.1 25.1 %all_to_all.26.recv = f32[16,8,128]{2,1,0:T(8,128)S(1)} all-to-all(f32[16,8,128]{2,1,0:T(8,128)S(1)} %plane_sum.1), channel_id=1, replica_groups=mesh['z'=16,'x'=4,'y'=4,'core'=2] {'z'}, dimensions={0} | all-to-all | bytes 131072 | tf_op jit(solution)/shard_map/all_to_all | solution.py:118
  63.2 15.9 %all_to_all.27.column = bf16[16,5,8,128]{3,2,1,0:T(8,128)(2,1)S(1)} all-to-all(bf16[16,5,8,128]{3,2,1,0:T(8,128)(2,1)S(1)} %get-tuple-element.10), channel_id=1, replica_groups=mesh['z'=16,'x'=4,'y'=4,'core'=2] {'z'}, dimensions={0} | all-to-all | bytes 327680 | tf_op jit(solution)/shard_map/all_to_all | solution.py:118
  79.1 0.1 column_squares.1
  79.2 15.4 %all_to_all.28.pieces = f32[32,8,128]{2,1,0:T(8,128)S(1)} all-to-all(f32[32,8,128]{2,1,0:T(8,128)S(1)} %column_squares.1), channel_id=1, replica_groups=mesh['z'=16,'x'=4,'y'=4,'core'=2] {'x','y','core'}, dimensions={0} | all-to-all | bytes 262144 | tf_op jit(solution)/shard_map/all_to_all | solution.py:118
  94.6 1.4 %plane_update.1 = (bf16[32,16,8,128]{3,2,1,0:T(8,128)(2,1)}, f32[8,128]{1,0:T(8,128)S(1)}) custom-call(f32[32,8,128]{2,1,0:T(8,128)S(1)} %all_to_all.28.pieces, bf16[16,5,8,128]{3,2,1,0:T(8,128)(2,1)S(1)} %all_to_all.27.column), custom_call_target="tpu_custom_call" | custom-call | tf_op jit(solution)/shard_map/plane_update/pallas_call | solution.py:151
  96.0 4.1 %all-to-all-start.4 = ((bf16[32,16,8,128]{3,2,1,0:T(8,128)(2,1)}), bf16[32,16,8,128]{3,2,1,0:T(8,128)(2,1)S(1)}, u32[]{:S(2)}, u32[]{:S(2)}) async-start(bf16[32,16,8,128]{3,2,1,0:T(8,128)(2,1)} %get-tuple-element.13), calls=%async_computation.4 | async-start | bytes 2097152 | tf_op jit(solution)/shard_map/all_to_all | solution.py:118
  100.1 1.9 %convolution_convert_fusion = bf16[4,99,2,512]{3,1,2,0:T(8,128)(2,1)S(1)} fusion(bf16[1,2,512,512]{3,1,2,0:T(2,128)(2,1)} %bitcast.98, f32[4,99,512]{2,1,0:T(8,128)S(1)} %copy-done.4, f32[4,99]{1,0:T(4,128)S(1)} %negate_multiply_fusion.1), kind=kOutput, calls=%fused_computation.1 | convolution fusion | flops 416047104 | bytes 2672176 | tf_op jit(solution)/shard_map/bfo,koi->bfki/dot_general | solution.py:33
  102.0 0.6 copy.24
  102.6 1.2 %concatenate.3 = bf16[4,199,512]{2,0,1:T(4,128)(2,1)} pad(bf16[4,198,512]{2,0,1:T(4,128)(2,1)S(1)} %bitcast.89, bf16[]{:T(256)} %constant.46.clone.1), padding=0_0x0_1x0_0 | pad | bytes 1626114 | tf_op jit(solution)/shard_map/concatenate | solution.py:38
  103.9 0.6 multiply_subtract_fusion
  104.5 12.6 %all-to-all-done.4 = bf16[32,16,8,128]{3,2,1,0:T(8,128)(2,1)S(1)} async-done(((bf16[32,16,8,128]{3,2,1,0:T(8,128)(2,1)}), bf16[32,16,8,128]{3,2,1,0:T(8,128)(2,1)S(1)}, u32[]{:S(2)}, u32[]{:S(2)}) %all-to-all-start.4) | async-done | bytes 1048608 | tf_op jit(solution)/shard_map/all_to_all | solution.py:118
  117.1 1.2 %copy.34 = bf16[16,32,8,128]{3,2,1,0:T(8,128)(2,1)} copy(bf16[16,32,8,128]{3,2,0,1:T(8,128)(2,1)S(1)} %bitcast.87) | data formatting | bytes 2097152 | tf_op jit(solution)/shard_map/transpose | solution.py:160
  (18 shorter events, 0.1 us)
Async XLA Ops:
  0.6 5.0 %copy-start = (bf16[512,1024]{1,0:T(8,128)(2,1)S(1)}, bf16[512,1024]{1,0:T(8,128)(2,1)}, u32[]{:S(2)}) copy-start(bf16[512,1024]{1,0:T(8,128)(2,1)} %param.13) | copy-start | bytes 3145732
  0.6 1.6 %copy-start.9 = (bf16[2,262144]{1,0:T(2,128)(2,1)S(1)}, bf16[2,262144]{1,0:T(2,128)(2,1)}, u32[]{:S(2)}) copy-start(bf16[2,262144]{1,0:T(2,128)(2,1)} %param.10) | copy-start | bytes 3145732
  2.2 0.9 copy-start.5
  2.3 1.2 copy-start.6
  2.3 1.2 copy-start.7
  3.4 2.3 %copy-start.8 = (f32[4,1024]{1,0:T(4,128)S(1)}, f32[4,1024]{1,0:T(4,128)}, u32[]{:S(2)}) copy-start(f32[4,1024]{1,0:T(4,128)} %param.14) | copy-start | bytes 49156
  37.9 25.3 %copy-start.1 = (f32[2,512]{1,0:T(2,128)S(1)}, f32[2,512]{1,0:T(2,128)}, u32[]{:S(2)}) copy-start(f32[2,512]{1,0:T(2,128)} %param.15) | copy-start | bytes 12292
  37.9 25.3 %copy-start.2 = (f32[2,512]{1,0:T(2,128)S(1)}, f32[2,512]{1,0:T(2,128)}, u32[]{:S(2)}) copy-start(f32[2,512]{1,0:T(2,128)} %param.16) | copy-start | bytes 12292
  37.9 25.3 %copy-start.3 = (f32[2,512]{1,0:T(2,128)S(1)}, f32[2,512]{1,0:T(2,128)}, u32[]{:S(2)}) copy-start(f32[2,512]{1,0:T(2,128)} %param.17) | copy-start | bytes 12292
  96.0 4.1 %copy-start.4 = (f32[4,99,512]{2,1,0:T(8,128)S(1)}, f32[4,99,512]{2,1,0:T(8,128)}, u32[]{:S(2)}) copy-start(f32[4,99,512]{2,1,0:T(8,128)} %get-tuple-element.19) | copy-start | bytes 2433028
  96.0 21.1 %all-to-all-start.4 = ((bf16[32,16,8,128]{3,2,1,0:T(8,128)(2,1)}), bf16[32,16,8,128]{3,2,1,0:T(8,128)(2,1)S(1)}, u32[]{:S(2)}, u32[]{:S(2)}) async-start(bf16[32,16,8,128]{3,2,1,0:T(8,128)(2,1)} %get-tuple-element.13), calls=%async_computation.4 | async-start | bytes 2097152 | tf_op jit(solution)/shard_map/all_to_all | solution.py:118

commit v5 on v4

--- a/solution.py
+++ b/solution.py
@@ -44,7 +44,7 @@
 LIMIT = 4 * 2**20
 
 
-def plane_sum(recv, out):
+def plane_sum(recv, master, first, second, out, rows):
     peers, taps, depth, width = recv.shape
     parts = width // LANES
     for tap in range(taps):
@@ -52,24 +52,22 @@
         for src in range(1, peers):
             total += recv[src, tap].astype(jnp.float32)
         for part in range(parts):
-            out[:, part * taps + tap, :] = total[:, part * LANES : (part + 1) * LANES]
+            rows[:, part * taps + tap, :] = total[:, part * LANES : (part + 1) * LANES]
+    out[0:depth] = rows[...].astype(jnp.bfloat16)
+    high = master[...].astype(jnp.bfloat16)
+    out[depth] = high
+    out[depth + 1] = (master[...] - high.astype(jnp.float32)).astype(jnp.bfloat16)
+    out[depth + 2] = first[...].astype(jnp.bfloat16)
+    out[depth + 3] = second[...].astype(jnp.bfloat16)
 
 
-def column_pack(recv, master, first, second, grad, out):
-    total = jnp.sum(recv[...], axis=0)
+def column_sum(column, grad, piece):
+    depth = column.shape[0]
+    total = column[0, 0:depth].astype(jnp.float32)
+    for src in range(1, depth):
+        total += column[src, 0:depth].astype(jnp.float32)
     grad[...] = total
-    high = master[...].astype(jnp.bfloat16)
-    low = (master[...] - high.astype(jnp.float32)).astype(jnp.bfloat16)
-    rows = (total.astype(jnp.bfloat16), high, low)
-    rows += (first[...].astype(jnp.bfloat16), second[...].astype(jnp.bfloat16))
-    for index, row in enumerate(rows):
-        for peer in range(out.shape[0]):
-            out[peer, index] = row
-
-
-def column_squares(column, piece):
-    grad = column[:, 0].astype(jnp.float32)
-    squares = jnp.sum(grad * grad, axis=0)
+    squares = jnp.sum(total * total, axis=0)
     squares = jnp.sum(jnp.sum(squares, axis=0, keepdims=True), axis=1, keepdims=True)
     piece[...] = jnp.broadcast_to(squares[None], piece.shape)
 
@@ -83,12 +81,14 @@
     return update, new_master, new_first, new_second
 
 
-def plane_update(pieces, column, out, scale_out, block, sems):
+def plane_update(pieces, grad, column, out, scale_out, block, sems):
+    depth = column.shape[0]
     squares = jnp.sum(pieces[...], axis=0)[0:1, 0:1]
     scale = jnp.minimum(1.0, 1.0 / (jnp.sqrt(squares) + 1e-06))
     scale_out[...] = jnp.broadcast_to(scale, scale_out.shape)
-    grad, high, low, first, second = (column[:, i].astype(jnp.float32) for i in range(5))
-    block[...] = advance(scale[None], grad, high + low, first, second)[1].astype(jnp.bfloat16)
+    high, low, first, second = (column[:, depth + i].astype(jnp.float32) for i in range(4))
+    new_master = advance(scale[None], grad[...], high + low, first, second)[1]
+    block[...] = new_master.astype(jnp.bfloat16)
     copies = [
         pltpu.make_async_copy(block, out.at[peer], sems.at[peer]) for peer in range(out.shape[0])
     ]
@@ -136,25 +136,27 @@
     f32, bf16 = jnp.float32, jnp.bfloat16
     shape = jax.ShapeDtypeStruct
     windows, dpre, input_grad = local_pass(inputs, weights, ln_gain, ln_bias, projection, targets)
-    order = jnp.arange(width).reshape(depth, plane).T.reshape(-1)
-    pick = (jnp.arange(width)[:, None] == order[None, :]).astype(bf16)
-    moved = jnp.einsum("bfo,op->bfp", dpre, pick, preferred_element_type=f32).astype(bf16)
-    term = jnp.einsum("bfo,bfki->koi", moved, windows, preferred_element_type=f32).astype(bf16)
-    term = term.reshape(taps, plane, depth, width).transpose(1, 0, 2, 3)
-    part = local(plane_sum, shape((depth,) + tile, f32), 1)(exchange(term, PLANE))
+    term = jnp.einsum("bfo,bfki->koi", dpre, windows, preferred_element_type=f32).astype(bf16)
+    term = term.reshape(taps, depth, plane, width).transpose(2, 0, 1, 3)
     shards = [to_rows(value) for value in (master, first_moment, second_moment)]
-    grad, packed = local(
-        column_pack, (shape(tile, f32), shape((depth, 5) + tile, bf16)), 4, (VMEM, VMEM)
-    )(exchange(part, "z"), *shards)
-    column = exchange(packed, "z")
-    piece = local(column_squares, shape((plane, 8, LANES), f32), 1)(column)
+    packed = local(
+        plane_sum, shape((depth + 4,) + tile, bf16), 4, VMEM, (pltpu.VMEM((depth,) + tile, f32),)
+    )(exchange(term, PLANE), *shards)
+    column = lax.all_gather(packed, "z")
+    grad, piece = local(
+        column_sum,
+        (shape((depth,) + tile, f32), shape((plane, 8, LANES), f32)),
+        1,
+        (VMEM, VMEM),
+    )(column)
     rows, scale = local(
         plane_update,
         (shape((plane, depth) + tile, bf16), shape((8, LANES), f32)),
-        2,
+        3,
         (ANY, VMEM),
         (pltpu.VMEM((depth,) + tile, bf16), pltpu.SemaphoreType.DMA((plane,))),
-    )(exchange(piece, PLANE), column)
+    )(exchange(piece, PLANE), grad, column)
+    grad = lax.dynamic_index_in_dim(grad, lax.axis_index("z"), 0, keepdims=False)
     fresh = [from_rows(value, taps) for value in advance(scale, grad, *shards)]
     update, new_master, new_first, new_second = fresh
     whole = exchange(rows, PLANE).transpose(1, 0, 2, 3)

time: 119 us -> 110 us (0.924)
  blocking collectives: 82.9 us -> 76.2 us
  matrix products: 5.73 us -> 4.06 us
    all_to_all x4 -> x2, blocking collectives: 82.9 us -> 45.3 us  [exchange(): return lax.all_to_all(value, axes, 0, 0, tiled=False)]
    all_gather x0 -> x1, blocking collectives: none -> 30.9 us  [body(): column = lax.all_gather(packed, 'z')]
    dot_general x1, matrix products: 2.58 us -> 0.92 us  [body(): jnp.einsum('bfo,bfki->koi', dpre, windows, preferred_element_type=f32)]
where the time goes in v5:
time: 110 us
  blocking collectives  76.2 us (69%)
  waiting for transfers between devices  12.6 us (11%)
  local copies, waits for them, and re-layouts  5.68 us (5%)
  other arithmetic  4.68 us (4%)
  starting transfers between devices  4.12 us (4%)
  matrix products  4.06 us (4%)
  Pallas kernels  1.72 us (2%)
    all_to_all x2, blocking collectives, exchange(): return lax.all_to_all(value, axes, 0, 0, tiled=False)  45.3 us
    all_gather x1, blocking collectives, body(): column = lax.all_gather(packed, 'z')  30.9 us
    all_to_all x1, waiting for transfers between devices, exchange(): return lax.all_to_all(value, axes, 0, 0, tiled=False)  12.6 us
    all_to_all x1, starting transfers between devices, exchange(): return lax.all_to_all(value, axes, 0, 0, tiled=False)  4.12 us
    reduce_sum x1, other arithmetic, local_pass(): pooled = jnp.mean(act, axis=1).astype(jnp.bfloat16)  2.23 us
  transfers between devices with their start and end apart: 1, of which 1 were waited for; matrix products, arithmetic and copies ran while one was open for 4% of the time, Pallas kernels for 0%

profile of v5, /device:TPU:1, one launch (start us, length us, event | category | flops | bytes accessed | tf_op | source)
XLA Modules:
  0.0 110.0 jit_solution(13622669472278015039)
XLA Ops:
  0.6 0.0 copy-start
  0.6 0.0 copy-start.11
  0.7 1.6 %slice.3 = bf16[4,198,512]{2,0,1:T(4,128)(2,1)S(1)} slice(bf16[4,199,512]{2,0,1:T(4,128)(2,1)} %param.9), slice={[0:4], [0:198], [0:512]} | slice | bytes 1622016 | tf_op jit(solution)/shard_map/slice | solution.py:21
  2.2 0.0 copy-start.6
  2.3 0.0 copy-start.8
  2.3 0.0 copy-start.9
  2.3 0.8 fusion.25
  3.0 0.1 copy-done.6
  3.1 0.3 multiply_reduce_fusion.2
  3.4 0.0 copy-start.10
  3.4 2.2 %multiply_reduce_fusion.1 = (f32[4,512]{1,0:T(4,128)S(1)}, f32[4,99,512]{2,1,0:T(8,128)S(1)}) fusion(f32[4,99,512]{2,1,0:T(8,128)S(1)} %get-tuple-element.25, f32[512]{0:T(512)S(1)} %copy-done.8, f32[512]{0:T(512)S(1)} %copy-done.9, f32[4,99]{1,0:T(4,128)S(1)} %fusion.19, f32[4,99]{1,0:T(4,128)S(1)} %broadcast_multiply_fusion.2), kind=kLoop, calls=%fused_computation.19 | loop fusion | flops 13987840 | bytes 1637472 | tf_op jit(solution)/shard_map/reduce_sum | solution.py:25
  5.7 0.5 broadcast_multiply_fusion
  6.2 0.7 multiply_reduce_fusion
  7.0 0.0 copy-start.7
  7.0 0.8 fusion.23
  7.8 0.3 copy-done.7
  8.1 0.9 bitcast_convert_fusion
  9.0 0.6 copy.68
  9.6 0.0 copy-start.3
  9.7 26.6 %all_to_all.15.recv = bf16[32,2,16,512]{3,2,1,0:T(8,128)(2,1)S(1)} all-to-all(bf16[32,2,16,512]{3,2,1,0:T(8,128)(2,1)S(1)} %bitcast.92), channel_id=1, replica_groups=mesh['z'=16,'x'=4,'y'=4,'core'=2] {'x','y','core'}, dimensions={0} | all-to-all | bytes 2097152 | tf_op jit(solution)/shard_map/all_to_all | solution.py:118
  36.3 0.2 plane_sum.1
  36.5 30.9 %all-gather = bf16[320,8,128]{2,1,0:T(8,128)(2,1)S(1)} all-gather(bf16[20,8,128]{2,1,0:T(8,128)(2,1)S(1)} %plane_sum.1), channel_id=2, replica_groups=mesh['z'=16,'x'=4,'y'=4,'core'=2] {'z'}, dimensions={0}, use_global_device_ids=true | all-gather | bytes 696320 | tf_op jit(solution)/shard_map/all_gather | solution.py:145
  67.4 0.2 column_sum.1
  67.5 18.7 %all_to_all.16.pieces = f32[32,8,128]{2,1,0:T(8,128)S(1)} all-to-all(f32[32,8,128]{2,1,0:T(8,128)S(1)} %get-tuple-element.10), channel_id=1, replica_groups=mesh['z'=16,'x'=4,'y'=4,'core'=2] {'x','y','core'}, dimensions={0} | all-to-all | bytes 262144 | tf_op jit(solution)/shard_map/all_to_all | solution.py:118
  86.2 1.4 %plane_update.1 = (bf16[32,16,8,128]{3,2,1,0:T(8,128)(2,1)}, f32[8,128]{1,0:T(8,128)S(1)}) custom-call(f32[32,8,128]{2,1,0:T(8,128)S(1)} %all_to_all.16.pieces, f32[16,8,128]{2,1,0:T(8,128)S(1)} %get-tuple-element.11.grad, bf16[16,20,8,128]{3,2,1,0:T(8,128)(2,1)S(1)} %bitcast.84), custom_call_target="tpu_custom_call" | custom-call | tf_op jit(solution)/shard_map/plane_update/pallas_call | solution.py:152
  87.6 4.1 %all-to-all-start.2 = ((bf16[32,16,8,128]{3,2,1,0:T(8,128)(2,1)}), bf16[32,16,8,128]{3,2,1,0:T(8,128)(2,1)S(1)}, u32[]{:S(2)}, u32[]{:S(2)}) async-start(bf16[32,16,8,128]{3,2,1,0:T(8,128)(2,1)} %get-tuple-element.13), calls=%async_computation.2 | async-start | bytes 2097152 | tf_op jit(solution)/shard_map/all_to_all | solution.py:118
  91.8 1.9 %convolution_convert_fusion = bf16[4,99,2,512]{3,1,2,0:T(8,128)(2,1)S(1)} fusion(bf16[1,2,512,512]{3,1,2,0:T(2,128)(2,1)} %bitcast.102, f32[4,99,512]{2,1,0:T(8,128)S(1)} %copy-done.5, f32[4,99]{1,0:T(4,128)S(1)} %negate_multiply_fusion.1), kind=kOutput, calls=%fused_computation.1 | convolution fusion | flops 416047104 | bytes 2672176 | tf_op jit(solution)/shard_map/bfo,koi->bfki/dot_general | solution.py:33
  93.6 0.6 copy.36
  94.3 1.2 %concatenate.3 = bf16[4,199,512]{2,0,1:T(4,128)(2,1)} pad(bf16[4,198,512]{2,0,1:T(4,128)(2,1)S(1)} %bitcast.93, bf16[]{:T(256)} %constant.48.clone.1), padding=0_0x0_1x0_0 | pad | bytes 1626114 | tf_op jit(solution)/shard_map/concatenate | solution.py:38
  95.5 0.6 multiply_subtract_fusion
  96.1 12.6 %all-to-all-done.2 = bf16[32,16,8,128]{3,2,1,0:T(8,128)(2,1)S(1)} async-done(((bf16[32,16,8,128]{3,2,1,0:T(8,128)(2,1)}), bf16[32,16,8,128]{3,2,1,0:T(8,128)(2,1)S(1)}, u32[]{:S(2)}, u32[]{:S(2)}) %all-to-all-start.2) | async-done | bytes 1048608 | tf_op jit(solution)/shard_map/all_to_all | solution.py:118
  108.7 1.2 %copy.46 = bf16[16,32,8,128]{3,2,1,0:T(8,128)(2,1)} copy(bf16[16,32,8,128]{3,2,0,1:T(8,128)(2,1)S(1)} %bitcast.91) | data formatting | bytes 2097152 | tf_op jit(solution)/shard_map/transpose | solution.py:162
  (18 shorter events, 0.1 us)
Async XLA Ops:
  0.6 5.0 %copy-start = (bf16[512,1024]{1,0:T(8,128)(2,1)S(1)}, bf16[512,1024]{1,0:T(8,128)(2,1)}, u32[]{:S(2)}) copy-start(bf16[512,1024]{1,0:T(8,128)(2,1)} %param.13) | copy-start | bytes 3145732
  0.6 1.6 %copy-start.11 = (bf16[2,262144]{1,0:T(2,128)(2,1)S(1)}, bf16[2,262144]{1,0:T(2,128)(2,1)}, u32[]{:S(2)}) copy-start(bf16[2,262144]{1,0:T(2,128)(2,1)} %param.10) | copy-start | bytes 3145732
  2.2 0.9 copy-start.6
  2.3 1.2 %copy-start.8 = (f32[512]{0:T(512)S(1)}, f32[512]{0:T(512)}, u32[]{:S(2)}) copy-start(f32[512]{0:T(512)} %param.12) | copy-start | bytes 6148
  2.3 1.2 %copy-start.9 = (f32[512]{0:T(512)S(1)}, f32[512]{0:T(512)}, u32[]{:S(2)}) copy-start(f32[512]{0:T(512)} %param.11) | copy-start | bytes 6148
  3.4 2.3 %copy-start.10 = (f32[4,1024]{1,0:T(4,128)S(1)}, f32[4,1024]{1,0:T(4,128)}, u32[]{:S(2)}) copy-start(f32[4,1024]{1,0:T(4,128)} %param.14) | copy-start | bytes 49156
  7.0 1.1 %copy-start.7 = (bf16[4,198,512]{2,0,1:T(4,128)(2,1)S(1)}, bf16[4,198,512]{2,0,1:T(4,128)(2,1)}, u32[]{:S(2)}) copy-start(bf16[4,198,512]{2,0,1:T(4,128)(2,1)} %copy-done.6) | copy-start | bytes 2433028
  7.8 1.2 %copy-start.4 = (f32[4,99,512]{2,1,0:T(8,128)}, f32[4,99,512]{2,1,0:T(8,128)S(1)}, u32[]{:S(2)}) copy-start(f32[4,99,512]{2,1,0:T(8,128)S(1)} %get-tuple-element.19) | copy-start | bytes 2433028
  9.6 26.7 %copy-start.1 = (f32[2,512]{1,0:T(2,128)S(1)}, f32[2,512]{1,0:T(2,128)}, u32[]{:S(2)}) copy-start(f32[2,512]{1,0:T(2,128)} %param.15) | copy-start | bytes 12292
  9.6 26.7 %copy-start.2 = (f32[2,512]{1,0:T(2,128)S(1)}, f32[2,512]{1,0:T(2,128)}, u32[]{:S(2)}) copy-start(f32[2,512]{1,0:T(2,128)} %param.16) | copy-start | bytes 12292
  9.6 26.7 %copy-start.3 = (f32[2,512]{1,0:T(2,128)S(1)}, f32[2,512]{1,0:T(2,128)}, u32[]{:S(2)}) copy-start(f32[2,512]{1,0:T(2,128)} %param.17) | copy-start | bytes 12292
  87.6 4.1 %copy-start.5 = (f32[4,99,512]{2,1,0:T(8,128)S(1)}, f32[4,99,512]{2,1,0:T(8,128)}, u32[]{:S(2)}) copy-start(f32[4,99,512]{2,1,0:T(8,128)} %copy-done.4) | copy-start | bytes 2433028
  87.6 21.1 %all-to-all-start.2 = ((bf16[32,16,8,128]{3,2,1,0:T(8,128)(2,1)}), bf16[32,16,8,128]{3,2,1,0:T(8,128)(2,1)S(1)}, u32[]{:S(2)}, u32[]{:S(2)}) async-start(bf16[32,16,8,128]{3,2,1,0:T(8,128)(2,1)} %get-tuple-element.13), calls=%async_computation.2 | async-start | bytes 2097152 | tf_op jit(solution)/shard_map/all_to_all | solution.py:118

commit v6 on v5

--- a/solution.py
+++ b/solution.py
@@ -81,16 +81,23 @@
     return update, new_master, new_first, new_second
 
 
-def plane_update(pieces, grad, column, out, scale_out, block, sems):
+def plane_update(pieces, grad, column, out, scale_out):
     depth = column.shape[0]
     squares = jnp.sum(pieces[...], axis=0)[0:1, 0:1]
     scale = jnp.minimum(1.0, 1.0 / (jnp.sqrt(squares) + 1e-06))
     scale_out[...] = jnp.broadcast_to(scale, scale_out.shape)
     high, low, first, second = (column[:, depth + i].astype(jnp.float32) for i in range(4))
     new_master = advance(scale[None], grad[...], high + low, first, second)[1]
-    block[...] = new_master.astype(jnp.bfloat16)
+    block = new_master.astype(jnp.bfloat16)
+    for peer in range(out.shape[0]):
+        out[peer] = block
+
+
+def place(core, source, *refs):
+    out, sems = refs[-2:]
     copies = [
-        pltpu.make_async_copy(block, out.at[peer], sems.at[peer]) for peer in range(out.shape[0])
+        pltpu.make_async_copy(source.at[:, z], out.at[z, :, core[0]], sems.at[z])
+        for z in range(out.shape[0])
     ]
     for copy in copies:
         copy.start()
@@ -99,6 +106,7 @@
 
 
 VMEM = pl.BlockSpec(memory_space=pltpu.VMEM)
+SMEM = pl.BlockSpec(memory_space=pltpu.SMEM)
 ANY = pl.BlockSpec(memory_space=pl.ANY)
 
 
@@ -112,6 +120,22 @@
         compiler_params=pltpu.CompilerParams(vmem_limit_bytes=LIMIT),
         name=kernel.__name__,
     )
+
+
+def put_half(core, half, whole=None):
+    peers, depth, *tile = half.shape
+    size = half.size * half.dtype.itemsize
+    return pl.pallas_call(
+        place,
+        out_shape=jax.ShapeDtypeStruct((depth, peers, 2, *tile), half.dtype),
+        in_specs=[SMEM, VMEM] + [ANY] * (whole is not None),
+        out_specs=ANY,
+        scratch_shapes=[pltpu.SemaphoreType.DMA((depth,))],
+        input_output_aliases={2: 0} if whole is not None else {},
+        compiler_params=pltpu.CompilerParams(vmem_limit_bytes=LIMIT),
+        cost_estimate=pl.CostEstimate(flops=0, transcendentals=0, bytes_accessed=2 * size),
+        name="put_half",
+    )(core, half, *(() if whole is None else (whole,)))
 
 
 def exchange(value, axes):
@@ -138,10 +162,11 @@
     windows, dpre, input_grad = local_pass(inputs, weights, ln_gain, ln_bias, projection, targets)
     term = jnp.einsum("bfo,bfki->koi", dpre, windows, preferred_element_type=f32).astype(bf16)
     term = term.reshape(taps, depth, plane, width).transpose(2, 0, 1, 3)
+    recv, input_grad = lax.optimization_barrier((exchange(term, PLANE), input_grad))
     shards = [to_rows(value) for value in (master, first_moment, second_moment)]
     packed = local(
         plane_sum, shape((depth + 4,) + tile, bf16), 4, VMEM, (pltpu.VMEM((depth,) + tile, f32),)
-    )(exchange(term, PLANE), *shards)
+    )(recv, *shards)
     column = lax.all_gather(packed, "z")
     grad, piece = local(
         column_sum,
@@ -151,15 +176,18 @@
     )(column)
     rows, scale = local(
         plane_update,
-        (shape((plane, depth) + tile, bf16), shape((8, LANES), f32)),
+        (shape((plane // 2, depth) + tile, bf16), shape((8, LANES), f32)),
         3,
-        (ANY, VMEM),
-        (pltpu.VMEM((depth,) + tile, bf16), pltpu.SemaphoreType.DMA((plane,))),
+        (VMEM, VMEM),
     )(exchange(piece, PLANE), grad, column)
     grad = lax.dynamic_index_in_dim(grad, lax.axis_index("z"), 0, keepdims=False)
     fresh = [from_rows(value, taps) for value in advance(scale, grad, *shards)]
     update, new_master, new_first, new_second = fresh
-    whole = exchange(rows, PLANE).transpose(1, 0, 2, 3)
+    own = exchange(rows, PLANE[:2])
+    other = lax.ppermute(own, "core", [(0, 1), (1, 0)])
+    core = lax.axis_index("core").reshape(1)
+    whole = put_half(core, own)
+    whole = put_half(1 - core, other, whole)
     new_weights = from_rows(whole, taps)
     return (input_grad, update, new_master, new_first, new_second, new_weights)
 

time: 110 us -> 107 us (0.973)
  blocking collectives: 76.2 us -> 61.9 us
  starting transfers between devices: 4.12 us -> 14.5 us
    all_to_all x2, blocking collectives: 45.3 us -> 31.8 us  [exchange(): return lax.all_to_all(value, axes, 0, 0, tiled=False)]
    all_to_all x1, starting transfers between devices: 4.12 us -> 10.6 us  [exchange(): return lax.all_to_all(value, axes, 0, 0, tiled=False)]
    ppermute x0 -> x1, starting transfers between devices: none -> 3.98 us  [body(): other = lax.ppermute(own, 'core', [(0, 1), (1, 0)])]
    transpose x1 -> x0, local copies, waits for them, and re-layouts: 1.24 us -> none  [body(): whole = exchange(rows, PLANE).transpose(1, 0, 2, 3)]
  transfers between devices with their start and end apart: 1 -> 2, of which waited for: 1 -> 1; matrix products, arithmetic and copies ran while one was open for 4% -> 4% of each run, Pallas kernels for 0% -> 1%
where the time goes in v6:
time: 107 us
  blocking collectives  61.9 us (58%)
  starting transfers between devices  14.5 us (14%)
  waiting for transfers between devices  13.2 us (12%)
  local copies, waits for them, and re-layouts  5.4 us (5%)
  other arithmetic  4.69 us (4%)
  matrix products  4.05 us (4%)
  Pallas kernels  2.36 us (2%)
    all_to_all x2, blocking collectives, exchange(): return lax.all_to_all(value, axes, 0, 0, tiled=False)  31.8 us
    all_gather x1, blocking collectives, body(): column = lax.all_gather(packed, 'z')  30.1 us
    all_to_all x1, waiting for transfers between devices, exchange(): return lax.all_to_all(value, axes, 0, 0, tiled=False)  13.2 us
    all_to_all x1, starting transfers between devices, exchange(): return lax.all_to_all(value, axes, 0, 0, tiled=False)  10.6 us
    ppermute x1, starting transfers between devices, body(): other = lax.ppermute(own, 'core', [(0, 1), (1, 0)])  3.98 us
    reduce_sum x1, other arithmetic, local_pass(): pooled = jnp.mean(act, axis=1).astype(jnp.bfloat16)  2.23 us
  transfers between devices with their start and end apart: 2, of which 1 were waited for; matrix products, arithmetic and copies ran while one was open for 4% of the time, Pallas kernels for 1%

profile of v6, /device:TPU:1, one launch (start us, length us, event | category | flops | bytes accessed | tf_op | source)
XLA Modules:
  0.0 107.1 jit_solution(7410840146996443484)
XLA Ops:
  0.6 0.0 copy-start
  0.6 0.0 copy-start.11
  0.7 1.6 %slice.3 = bf16[4,198,512]{2,0,1:T(4,128)(2,1)S(1)} slice(bf16[4,199,512]{2,0,1:T(4,128)(2,1)} %param.9), slice={[0:4], [0:198], [0:512]} | slice | bytes 1622016 | tf_op jit(solution)/shard_map/slice | solution.py:21
  2.2 0.0 copy-start.6
  2.3 0.0 copy-start.8
  2.3 0.8 fusion.25
  3.0 0.1 copy-done.6
  3.1 0.3 multiply_reduce_fusion.2
  3.4 2.2 %multiply_reduce_fusion.1 = (f32[4,512]{1,0:T(4,128)S(1)}, f32[4,99,512]{2,1,0:T(8,128)S(1)}) fusion(f32[4,99,512]{2,1,0:T(8,128)S(1)} %get-tuple-element.29, f32[512]{0:T(512)S(1)} %copy-done.8, f32[512]{0:T(512)S(1)} %copy-done.9, f32[4,99]{1,0:T(4,128)S(1)} %fusion.19, f32[4,99]{1,0:T(4,128)S(1)} %broadcast_multiply_fusion.2), kind=kLoop, calls=%fused_computation.19 | loop fusion | flops 13987840 | bytes 1637472 | tf_op jit(solution)/shard_map/reduce_sum | solution.py:25
  5.7 0.5 broadcast_multiply_fusion
  6.2 0.7 multiply_reduce_fusion
  7.0 0.8 fusion.23
  7.8 0.3 copy-done.7
  8.1 0.9 bitcast_convert_fusion
  9.0 1.5 %copy.70 = bf16[2,16,32,512]{3,1,0,2:T(8,128)(2,1)} copy(bf16[2,16,32,512]{3,2,1,0:T(8,128)(2,1)S(1)} %bitcast.93) | data formatting | bytes 2097152 | tf_op jit(solution)/shard_map/reshape | solution.py:164
  10.6 10.6 %all-to-all-start = ((bf16[32,2,16,512]{3,2,1,0:T(8,128)(2,1)}), bf16[32,2,16,512]{3,2,1,0:T(8,128)(2,1)S(1)}, u32[]{:S(2)}, u32[]{:S(2)}) async-start(bf16[32,2,16,512]{3,2,1,0:T(8,128)(2,1)} %bitcast.82), calls=%async_computation | async-start | bytes 2097152 | tf_op jit(solution)/shard_map/all_to_all | solution.py:142
  21.1 1.9 %convolution_convert_fusion = bf16[4,99,2,512]{3,1,2,0:T(8,128)(2,1)S(1)} fusion(bf16[1,2,512,512]{3,1,2,0:T(2,128)(2,1)} %bitcast.100, f32[4,99,512]{2,1,0:T(8,128)S(1)} %copy-done.5, f32[4,99]{1,0:T(4,128)S(1)} %negate_multiply_fusion.1), kind=kOutput, calls=%fused_computation.1 | convolution fusion | flops 416047104 | bytes 2672176 | tf_op jit(solution)/shard_map/bfo,koi->bfki/dot_general | solution.py:33
  23.0 0.6 copy.40
  23.7 0.0 copy-start.2
  23.7 0.0 copy-start.3
  23.7 1.2 %concatenate.3 = bf16[4,199,512]{2,0,1:T(4,128)(2,1)} pad(bf16[4,198,512]{2,0,1:T(4,128)(2,1)S(1)} %bitcast.92, bf16[]{:T(256)} %constant.48.clone.1), padding=0_0x0_1x0_0 | pad | bytes 1626114 | tf_op jit(solution)/shard_map/concatenate | solution.py:38
  24.9 13.2 %all-to-all-done.recv = bf16[32,2,16,512]{3,2,1,0:T(8,128)(2,1)S(1)} async-done(((bf16[32,2,16,512]{3,2,1,0:T(8,128)(2,1)}), bf16[32,2,16,512]{3,2,1,0:T(8,128)(2,1)S(1)}, u32[]{:S(2)}, u32[]{:S(2)}) %all-to-all-start) | async-done | bytes 1048608 | tf_op jit(solution)/shard_map/all_to_all | solution.py:142
  38.1 0.2 plane_sum.1
  38.3 30.1 %all-gather = bf16[320,8,128]{2,1,0:T(8,128)(2,1)S(1)} all-gather(bf16[20,8,128]{2,1,0:T(8,128)(2,1)S(1)} %plane_sum.1), channel_id=2, replica_groups=mesh['z'=16,'x'=4,'y'=4,'core'=2] {'z'}, dimensions={0}, use_global_device_ids=true | all-gather | bytes 696320 | tf_op jit(solution)/shard_map/all_gather | solution.py:170
  68.5 0.2 column_sum.1
  68.6 18.7 %all_to_all.15.pieces = f32[32,8,128]{2,1,0:T(8,128)S(1)} all-to-all(f32[32,8,128]{2,1,0:T(8,128)S(1)} %get-tuple-element.14), channel_id=1, replica_groups=mesh['z'=16,'x'=4,'y'=4,'core'=2] {'x','y','core'}, dimensions={0} | all-to-all | bytes 262144 | tf_op jit(solution)/shard_map/all_to_all | solution.py:142
  87.4 0.2 plane_update.1
  87.5 13.1 %all_to_all.16.source = bf16[16,16,8,128]{3,2,1,0:T(8,128)(2,1)S(1)} all-to-all(bf16[16,16,8,128]{3,2,1,0:T(8,128)(2,1)S(1)} %get-tuple-element.17), channel_id=1, replica_groups=mesh['z'=16,'x'=4,'y'=4,'core'=2] {'x','y'}, dimensions={0} | all-to-all | bytes 1048576 | tf_op jit(solution)/shard_map/all_to_all | solution.py:142
  100.6 4.0 %collective-permute-start = (bf16[16,16,8,128]{3,2,1,0:T(8,128)(2,1)S(1)}, bf16[16,16,8,128]{3,2,1,0:T(8,128)(2,1)S(1)}, u32[]{:S(2)}, u32[]{:S(2)}) collective-permute-start(bf16[16,16,8,128]{3,2,1,0:T(8,128)(2,1)S(1)} %all_to_all.16.source), channel_id=1, source_target_pairs={{0,1},{1,0},{2,3},{3,2},{4,5},{5,4},{6,7},{7,6},{8,9},{9,8},{10,11... | collective-permute-start | bytes 1572872 | tf_op jit(solution)/shard_map/ppermute | solution.py:187
  104.6 0.6 multiply_subtract_fusion
  105.2 0.9 put_half.2.refs_0_
  106.1 0.9 put_half.3
  (21 shorter events, 0.1 us)
Async XLA Ops:
  0.6 5.0 %copy-start = (bf16[512,1024]{1,0:T(8,128)(2,1)S(1)}, bf16[512,1024]{1,0:T(8,128)(2,1)}, u32[]{:S(2)}) copy-start(bf16[512,1024]{1,0:T(8,128)(2,1)} %param.13) | copy-start | bytes 3145732
  0.6 1.6 %copy-start.11 = (bf16[2,262144]{1,0:T(2,128)(2,1)S(1)}, bf16[2,262144]{1,0:T(2,128)(2,1)}, u32[]{:S(2)}) copy-start(bf16[2,262144]{1,0:T(2,128)(2,1)} %param.10) | copy-start | bytes 3145732
  2.2 0.9 copy-start.6
  2.3 1.2 %copy-start.8 = (f32[512]{0:T(512)S(1)}, f32[512]{0:T(512)}, u32[]{:S(2)}) copy-start(f32[512]{0:T(512)} %param.12) | copy-start | bytes 6148
  2.3 1.2 %copy-start.9 = (f32[512]{0:T(512)S(1)}, f32[512]{0:T(512)}, u32[]{:S(2)}) copy-start(f32[512]{0:T(512)} %param.11) | copy-start | bytes 6148
  3.4 2.3 %copy-start.10 = (f32[4,1024]{1,0:T(4,128)S(1)}, f32[4,1024]{1,0:T(4,128)}, u32[]{:S(2)}) copy-start(f32[4,1024]{1,0:T(4,128)} %param.14) | copy-start | bytes 49156
  6.9 1.2 %copy-start.7 = (bf16[4,198,512]{2,0,1:T(4,128)(2,1)S(1)}, bf16[4,198,512]{2,0,1:T(4,128)(2,1)}, u32[]{:S(2)}) copy-start(bf16[4,198,512]{2,0,1:T(4,128)(2,1)} %copy-done.6) | copy-start | bytes 2433028
  7.8 1.2 %copy-start.4 = (f32[4,99,512]{2,1,0:T(8,128)}, f32[4,99,512]{2,1,0:T(8,128)S(1)}, u32[]{:S(2)}) copy-start(f32[4,99,512]{2,1,0:T(8,128)S(1)} %get-tuple-element.23) | copy-start | bytes 2433028
  10.6 10.6 %copy-start.5 = (f32[4,99,512]{2,1,0:T(8,128)S(1)}, f32[4,99,512]{2,1,0:T(8,128)}, u32[]{:S(2)}) copy-start(f32[4,99,512]{2,1,0:T(8,128)} %copy-done.4) | copy-start | bytes 2433028
  10.6 27.6 %all-to-all-start = ((bf16[32,2,16,512]{3,2,1,0:T(8,128)(2,1)}), bf16[32,2,16,512]{3,2,1,0:T(8,128)(2,1)S(1)}, u32[]{:S(2)}, u32[]{:S(2)}) async-start(bf16[32,2,16,512]{3,2,1,0:T(8,128)(2,1)} %bitcast.82), calls=%async_computation | async-start | bytes 2097152 | tf_op jit(solution)/shard_map/all_to_all | solution.py:142
  23.7 14.5 %copy-start.1 = (f32[2,512]{1,0:T(2,128)S(1)}, f32[2,512]{1,0:T(2,128)}, u32[]{:S(2)}) copy-start(f32[2,512]{1,0:T(2,128)} %param.15) | copy-start | bytes 12292
  23.7 14.5 %copy-start.2 = (f32[2,512]{1,0:T(2,128)S(1)}, f32[2,512]{1,0:T(2,128)}, u32[]{:S(2)}) copy-start(f32[2,512]{1,0:T(2,128)} %param.16) | copy-start | bytes 12292
  23.7 14.5 %copy-start.3 = (f32[2,512]{1,0:T(2,128)S(1)}, f32[2,512]{1,0:T(2,128)}, u32[]{:S(2)}) copy-start(f32[2,512]{1,0:T(2,128)} %param.17) | copy-start | bytes 12292
  100.6 5.5 %collective-permute-start = (bf16[16,16,8,128]{3,2,1,0:T(8,128)(2,1)S(1)}, bf16[16,16,8,128]{3,2,1,0:T(8,128)(2,1)S(1)}, u32[]{:S(2)}, u32[]{:S(2)}) collective-permute-start(bf16[16,16,8,128]{3,2,1,0:T(8,128)(2,1)S(1)} %all_to_all.16.source), channel_id=1, source_target_pairs={{0,1},{1,0},{2,3},{3,2},{4,5},{5,4},{6,7},{7,6},{8,9},{9,8},{10,11... | collective-permute-start | bytes 1572872 | tf_op jit(solution)/shard_map/ppermute | solution.py:187

commit v7 on v6

--- a/solution.py
+++ b/solution.py
@@ -1,3 +1,5 @@
+import math
+
 import jax
 import jax.numpy as jnp
 from jax import lax
@@ -7,11 +9,48 @@
 from jax.sharding import PartitionSpec as P
 
 
-def norm_act(pre, gain, bias):
-    center = pre - jnp.mean(pre, axis=-1, keepdims=True)
-    spread = jnp.mean(center * center, axis=-1, keepdims=True)
-    normed = center * lax.rsqrt(spread + 1e-05)
-    return jax.nn.gelu(normed * gain + bias, approximate=False)
+AXES = ("z", "x", "y", "core")
+PLANE = ("x", "y", "core")
+LANES = 128
+LIMIT = 4 * 2**20
+VMEM = pl.BlockSpec(memory_space=pltpu.VMEM)
+
+
+def chunks(frames):
+    return [slice(start, min(start + 8, frames)) for start in range(0, frames, 8)]
+
+
+def middle(pre, gain, bias, projection, targets, dpre, normed, slope, deviation):
+    clips, frames, width = pre.shape
+    gains, biases = gain[...][None], bias[...][None]
+    pooled = jnp.zeros((clips, width), jnp.float32)
+    for rows in chunks(frames):
+        value = pre[:, rows, :]
+        center = value - jnp.mean(value, axis=-1, keepdims=True)
+        spread = jnp.mean(center * center, axis=-1, keepdims=True)
+        inverse = lax.rsqrt(spread + 1e-05)
+        normal = center * inverse
+        point = normal * gains + biases
+        share = 0.5 + 0.5 * lax.erf(point * math.sqrt(0.5))
+        bell = jnp.exp(-0.5 * point * point) * (1.0 / math.sqrt(2.0 * math.pi))
+        pooled += jnp.sum(point * share, axis=1)
+        normed[:, rows, :] = normal
+        slope[:, rows, :] = (share + point * bell) * gains
+        deviation[:, rows, :] = jnp.broadcast_to(inverse, inverse.shape[:2] + (LANES,))
+    pooled = (pooled / frames).astype(jnp.bfloat16)
+    predicted = jnp.dot(pooled, projection[...], preferred_element_type=jnp.float32)
+    miss = (predicted - targets[...]).astype(jnp.bfloat16)
+    back = lax.dot_general(
+        miss, projection[...], (((1,), (1,)), ((), ())), preferred_element_type=jnp.float32
+    )
+    upstream = (back / frames)[:, None, :]
+    for rows in chunks(frames):
+        normal = normed[:, rows, :]
+        grad = slope[:, rows, :] * upstream
+        first = jnp.mean(grad, axis=-1, keepdims=True)
+        second = jnp.mean(grad * normal, axis=-1, keepdims=True)
+        inverse = deviation[:, rows, 0:1]
+        dpre[:, rows, :] = (inverse * (grad - first - normal * second)).astype(jnp.bfloat16)
 
 
 def local_pass(inputs, weights, ln_gain, ln_bias, projection, targets):
@@ -21,27 +60,23 @@
     windows = inputs[:, : frames_out * taps].reshape(clips, frames_out, taps, chans)
     kernel = weights.reshape(taps, chans, chans)
     pre = jnp.einsum("bfki,koi->bfo", windows, kernel, preferred_element_type=jnp.float32)
-    act, pull = jax.vjp(lambda value: norm_act(value, ln_gain, ln_bias), pre)
-    pooled = jnp.mean(act, axis=1).astype(jnp.bfloat16)
-    predicted = jnp.dot(pooled, projection, preferred_element_type=jnp.float32)
-    miss = (predicted - targets).astype(jnp.bfloat16)
-    back = lax.dot_general(
-        miss, projection, (((1,), (1,)), ((), ())), preferred_element_type=jnp.float32
-    )
-    upstream = jnp.broadcast_to(back[:, None, :] / frames_out, act.shape)
-    dpre = pull(upstream)[0].astype(jnp.bfloat16)
+    dpre = local(
+        middle,
+        jax.ShapeDtypeStruct(pre.shape, jnp.bfloat16),
+        5,
+        VMEM,
+        (
+            pltpu.VMEM(pre.shape, jnp.float32),
+            pltpu.VMEM(pre.shape, jnp.float32),
+            pltpu.VMEM(pre.shape[:2] + (LANES,), jnp.float32),
+        ),
+    )(pre, ln_gain[None], ln_bias[None], projection, targets)
     dwin = jnp.einsum("bfo,koi->bfki", dpre, kernel, preferred_element_type=jnp.float32).astype(
         jnp.bfloat16
     )
     dinput = dwin.reshape(clips, frames_out * taps, chans)
     tail = jnp.zeros((clips, frames_in - frames_out * taps, chans), jnp.bfloat16)
     return (windows, dpre, jnp.concatenate([dinput, tail], axis=1))
-
-
-AXES = ("z", "x", "y", "core")
-PLANE = ("x", "y", "core")
-LANES = 128
-LIMIT = 4 * 2**20
 
 
 def plane_sum(recv, master, first, second, out, rows):
@@ -105,7 +140,6 @@
         copy.wait()
 
 
-VMEM = pl.BlockSpec(memory_space=pltpu.VMEM)
 SMEM = pl.BlockSpec(memory_space=pltpu.SMEM)
 ANY = pl.BlockSpec(memory_space=pl.ANY)
 
@@ -162,11 +196,10 @@
     windows, dpre, input_grad = local_pass(inputs, weights, ln_gain, ln_bias, projection, targets)
     term = jnp.einsum("bfo,bfki->koi", dpre, windows, preferred_element_type=f32).astype(bf16)
     term = term.reshape(taps, depth, plane, width).transpose(2, 0, 1, 3)
-    recv, input_grad = lax.optimization_barrier((exchange(term, PLANE), input_grad))
     shards = [to_rows(value) for value in (master, first_moment, second_moment)]
     packed = local(
         plane_sum, shape((depth + 4,) + tile, bf16), 4, VMEM, (pltpu.VMEM((depth,) + tile, f32),)
-    )(recv, *shards)
+    )(exchange(term, PLANE), *shards)
     column = lax.all_gather(packed, "z")
     grad, piece = local(
         column_sum,
@@ -174,12 +207,13 @@
         1,
         (VMEM, VMEM),
     )(column)
+    pieces, input_grad = lax.optimization_barrier((exchange(piece, PLANE), input_grad))
     rows, scale = local(
         plane_update,
         (shape((plane // 2, depth) + tile, bf16), shape((8, LANES), f32)),
         3,
         (VMEM, VMEM),
-    )(exchange(piece, PLANE), grad, column)
+    )(pieces, grad, column)
     grad = lax.dynamic_index_in_dim(grad, lax.axis_index("z"), 0, keepdims=False)
     fresh = [from_rows(value, taps) for value in advance(scale, grad, *shards)]
     update, new_master, new_first, new_second = fresh

time: 107 us -> 104 us (0.972)
  blocking collectives: 61.9 us -> 70.6 us
  waiting for transfers between devices: 13.2 us -> 5.21 us
  other arithmetic: 4.69 us -> 0.63 us
  Pallas kernels: 2.36 us -> 4.64 us
  matrix products: 4.05 us -> 2.08 us
    all_to_all x1, waiting for transfers between devices: 13.2 us -> 5.21 us  [exchange(): return lax.all_to_all(value, axes, 0, 0, tiled=False)]
    all_to_all x2, blocking collectives: 31.8 us -> 39.7 us  [exchange(): return lax.all_to_all(value, axes, 0, 0, tiled=False)]
    reduce_sum x4 -> x0, other arithmetic: 4.04 us -> none  [the longest x1 2.23 us: local_pass(): pooled = jnp.mean(act, axis=1).astype(jnp.bfloat16)]
    pallas_call x0 -> x1, Pallas kernels: none -> 1.63 us  [local_pass(): local(middle, jax.ShapeDtypeStruct(pre.shape, jnp.bfloat16), 5, VMEM, (pl...]
    dot_general x1, matrix products: 1.87 us -> 0.61 us  [local_pass(): jnp.einsum('bfo,koi->bfki', dpre, kernel, preferred_element_type=jnp.floa...]
  transfers between devices with their start and end apart: 2 -> 2, of which waited for: 1 -> 1; matrix products, arithmetic and copies ran while one was open for 4% -> 3% of each run, Pallas kernels for 1% -> 1%
where the time goes in v7:
time: 104 us
  blocking collectives  70.6 us (68%)
  starting transfers between devices  15.2 us (15%)
  waiting for transfers between devices  5.21 us (5%)
  Pallas kernels  4.64 us (4%)
  local copies, waits for them, and re-layouts  4.49 us (4%)
  matrix products  2.08 us (2%)
    all_to_all x2, blocking collectives, exchange(): return lax.all_to_all(value, axes, 0, 0, tiled=False)  39.7 us
    all_gather x1, blocking collectives, body(): column = lax.all_gather(packed, 'z')  30.9 us
    all_to_all x1, starting transfers between devices, exchange(): return lax.all_to_all(value, axes, 0, 0, tiled=False)  11.2 us
    all_to_all x1, waiting for transfers between devices, exchange(): return lax.all_to_all(value, axes, 0, 0, tiled=False)  5.21 us
    ppermute x1, starting transfers between devices, body(): other = lax.ppermute(own, 'core', [(0, 1), (1, 0)])  3.98 us
  transfers between devices with their start and end apart: 2, of which 1 were waited for; matrix products, arithmetic and copies ran while one was open for 3% of the time, Pallas kernels for 1%

profile of v7, /device:TPU:1, one launch (start us, length us, event | category | flops | bytes accessed | tf_op | source)
XLA Modules:
  0.0 103.6 jit_solution(6309521575383382220)
XLA Ops:
  0.6 0.0 copy-start.7
  0.6 1.5 %slice.3 = bf16[4,198,512]{2,0,1:T(4,128)(2,1)S(1)} slice(bf16[4,199,512]{2,0,1:T(4,128)(2,1)} %param.9), slice={[0:4], [0:198], [0:512]} | slice | bytes 1622016 | tf_op jit(solution)/shard_map/slice | solution.py:60
  2.2 0.0 copy-done.7
  2.2 0.0 copy-start
  2.2 0.0 copy-start.1
  2.2 0.0 copy-start.5
  2.2 0.0 copy-start.6
  2.2 0.7 convolution_bitcast_fusion.pre
  2.9 0.5 copy-done
  3.4 0.0 copy-done.5
  3.4 1.6 %middle.1 = bf16[4,99,512]{2,1,0:T(8,128)(2,1)S(1)} custom-call(f32[4,99,512]{2,1,0:T(8,128)S(1)} %convolution_bitcast_fusion.pre, f32[1,512]{1,0:T(1,128)S(1)} %bitcast.89, f32[1,512]{1,0:T(1,128)S(1)} %bitcast.90, bf16[512,1024]{1,0:T(8,128)(2,1)S(1)} %copy-done, f32[4,1024]{1,0:T(4,128)S(1)} %copy-done.1), custom_call_target="tpu_custom_call" | custom-call | tf_op jit(solution)/shard_map/middle/pallas_call | solution.py:63
  5.0 0.8 bitcast_convert_fusion
  5.9 0.6 copy.66
  6.4 0.0 copy-start.2
  6.5 0.0 copy-start.3
  6.5 0.0 copy-start.4
  6.5 26.6 %all_to_all.15.recv = bf16[32,2,16,512]{3,2,1,0:T(8,128)(2,1)S(1)} all-to-all(bf16[32,2,16,512]{3,2,1,0:T(8,128)(2,1)S(1)} %bitcast.92), channel_id=1, replica_groups=mesh['z'=16,'x'=4,'y'=4,'core'=2] {'x','y','core'}, dimensions={0} | all-to-all | bytes 2097152 | tf_op jit(solution)/shard_map/all_to_all | solution.py:176
  33.1 0.2 plane_sum.1
  33.3 30.9 %all-gather = bf16[320,8,128]{2,1,0:T(8,128)(2,1)S(1)} all-gather(bf16[20,8,128]{2,1,0:T(8,128)(2,1)S(1)} %plane_sum.1), channel_id=2, replica_groups=mesh['z'=16,'x'=4,'y'=4,'core'=2] {'z'}, dimensions={0}, use_global_device_ids=true | all-gather | bytes 696320 | tf_op jit(solution)/shard_map/all_gather | solution.py:203
  64.2 0.8 column_sum.1
  65.0 11.2 %all-to-all-start.1 = ((f32[32,8,128]{2,1,0:T(8,128)}), f32[32,8,128]{2,1,0:T(8,128)S(1)}, u32[]{:S(2)}, u32[]{:S(2)}) async-start(f32[32,8,128]{2,1,0:T(8,128)} %get-tuple-element.12), calls=%async_computation.1 | async-start | bytes 262144 | tf_op jit(solution)/shard_map/all_to_all | solution.py:176
  76.3 0.6 convolution_convert_fusion
  76.9 0.6 copy.43
  77.5 1.2 %concatenate.3 = bf16[4,199,512]{2,0,1:T(4,128)(2,1)} pad(bf16[4,198,512]{2,0,1:T(4,128)(2,1)S(1)} %bitcast.93, bf16[]{:T(256)} %constant.16.clone.1), padding=0_0x0_1x0_0 | pad | bytes 1626114 | tf_op jit(solution)/shard_map/concatenate | solution.py:79
  78.7 5.2 %all-to-all-done.1.pieces = f32[32,8,128]{2,1,0:T(8,128)S(1)} async-done(((f32[32,8,128]{2,1,0:T(8,128)}), f32[32,8,128]{2,1,0:T(8,128)S(1)}, u32[]{:S(2)}, u32[]{:S(2)}) %all-to-all-start.1) | async-done | bytes 131104 | tf_op jit(solution)/shard_map/all_to_all | solution.py:176
  83.9 0.2 plane_update.1
  84.1 13.1 %all_to_all.16.source = bf16[16,16,8,128]{3,2,1,0:T(8,128)(2,1)S(1)} all-to-all(bf16[16,16,8,128]{3,2,1,0:T(8,128)(2,1)S(1)} %get-tuple-element.17), channel_id=1, replica_groups=mesh['z'=16,'x'=4,'y'=4,'core'=2] {'x','y'}, dimensions={0} | all-to-all | bytes 1048576 | tf_op jit(solution)/shard_map/all_to_all | solution.py:176
  97.2 4.0 %collective-permute-start = (bf16[16,16,8,128]{3,2,1,0:T(8,128)(2,1)S(1)}, bf16[16,16,8,128]{3,2,1,0:T(8,128)(2,1)S(1)}, u32[]{:S(2)}, u32[]{:S(2)}) collective-permute-start(bf16[16,16,8,128]{3,2,1,0:T(8,128)(2,1)S(1)} %all_to_all.16.source), channel_id=1, source_target_pairs={{0,1},{1,0},{2,3},{3,2},{4,5},{5,4},{6,7},{7,6},{8,9},{9,8},{10,11... | collective-permute-start | bytes 1572872 | tf_op jit(solution)/shard_map/ppermute | solution.py:221
  101.2 0.6 multiply_subtract_fusion
  101.8 0.9 put_half.2.refs_0_
  102.7 0.0 collective-permute-done.source
  102.7 0.9 put_half.3
  (5 shorter events, 0.0 us)
Async XLA Ops:
  0.6 1.5 %copy-start.7 = (bf16[2,262144]{1,0:T(2,128)(2,1)S(1)}, bf16[2,262144]{1,0:T(2,128)(2,1)}, u32[]{:S(2)}) copy-start(bf16[2,262144]{1,0:T(2,128)(2,1)} %param.10) | copy-start | bytes 3145732
  2.2 1.2 %copy-start = (bf16[512,1024]{1,0:T(8,128)(2,1)S(1)}, bf16[512,1024]{1,0:T(8,128)(2,1)}, u32[]{:S(2)}) copy-start(bf16[512,1024]{1,0:T(8,128)(2,1)} %projection.1) | copy-start | bytes 3145732
  2.2 1.2 %copy-start.1 = (f32[4,1024]{1,0:T(4,128)S(1)}, f32[4,1024]{1,0:T(4,128)}, u32[]{:S(2)}) copy-start(f32[4,1024]{1,0:T(4,128)} %targets.1) | copy-start | bytes 49156
  2.2 1.2 %copy-start.5 = (f32[512]{0:T(512)S(1)}, f32[512]{0:T(512)}, u32[]{:S(2)}) copy-start(f32[512]{0:T(512)} %param.11) | copy-start | bytes 6148
  2.2 1.2 %copy-start.6 = (f32[512]{0:T(512)S(1)}, f32[512]{0:T(512)}, u32[]{:S(2)}) copy-start(f32[512]{0:T(512)} %param.12) | copy-start | bytes 6148
  6.4 26.7 %copy-start.2 = (f32[2,512]{1,0:T(2,128)S(1)}, f32[2,512]{1,0:T(2,128)}, u32[]{:S(2)}) copy-start(f32[2,512]{1,0:T(2,128)} %param.15) | copy-start | bytes 12292
  6.5 26.7 %copy-start.3 = (f32[2,512]{1,0:T(2,128)S(1)}, f32[2,512]{1,0:T(2,128)}, u32[]{:S(2)}) copy-start(f32[2,512]{1,0:T(2,128)} %param.16) | copy-start | bytes 12292
  6.5 26.7 %copy-start.4 = (f32[2,512]{1,0:T(2,128)S(1)}, f32[2,512]{1,0:T(2,128)}, u32[]{:S(2)}) copy-start(f32[2,512]{1,0:T(2,128)} %param.17) | copy-start | bytes 12292
  65.0 18.9 %all-to-all-start.1 = ((f32[32,8,128]{2,1,0:T(8,128)}), f32[32,8,128]{2,1,0:T(8,128)S(1)}, u32[]{:S(2)}, u32[]{:S(2)}) async-start(f32[32,8,128]{2,1,0:T(8,128)} %get-tuple-element.12), calls=%async_computation.1 | async-start | bytes 262144 | tf_op jit(solution)/shard_map/all_to_all | solution.py:176
  97.2 5.5 %collective-permute-start = (bf16[16,16,8,128]{3,2,1,0:T(8,128)(2,1)S(1)}, bf16[16,16,8,128]{3,2,1,0:T(8,128)(2,1)S(1)}, u32[]{:S(2)}, u32[]{:S(2)}) collective-permute-start(bf16[16,16,8,128]{3,2,1,0:T(8,128)(2,1)S(1)} %all_to_all.16.source), channel_id=1, source_target_pairs={{0,1},{1,0},{2,3},{3,2},{4,5},{5,4},{6,7},{7,6},{8,9},{9,8},{10,11... | collective-permute-start | bytes 1572872 | tf_op jit(solution)/shard_map/ppermute | solution.py:221

commit v8 on v7

--- a/solution.py
+++ b/solution.py
@@ -11,6 +11,7 @@
 
 AXES = ("z", "x", "y", "core")
 PLANE = ("x", "y", "core")
+SWAP = ((0, 1), (1, 0))
 LANES = 128
 LIMIT = 4 * 2**20
 VMEM = pl.BlockSpec(memory_space=pltpu.VMEM)
@@ -79,6 +80,12 @@
     return (windows, dpre, jnp.concatenate([dinput, tail], axis=1))
 
 
+def merge(core, term, recv, out):
+    for peer in range(out.shape[0]):
+        total = term[peer, core[0]].astype(jnp.float32) + recv[peer].astype(jnp.float32)
+        out[peer] = total.astype(jnp.bfloat16)
+
+
 def plane_sum(recv, master, first, second, out, rows):
     peers, taps, depth, width = recv.shape
     parts = width // LANES
@@ -196,10 +203,21 @@
     windows, dpre, input_grad = local_pass(inputs, weights, ln_gain, ln_bias, projection, targets)
     term = jnp.einsum("bfo,bfki->koi", dpre, windows, preferred_element_type=f32).astype(bf16)
     term = term.reshape(taps, depth, plane, width).transpose(2, 0, 1, 3)
+    term = lax.optimization_barrier(term).reshape(plane // 2, 2, taps, depth, width)
+    core = lax.axis_index("core").reshape(1)
+    away = lax.dynamic_index_in_dim(term, 1 - core[0], 1, keepdims=False)
+    term = pl.pallas_call(
+        merge,
+        out_shape=shape(away.shape, bf16),
+        in_specs=[SMEM, VMEM, VMEM],
+        out_specs=VMEM,
+        compiler_params=pltpu.CompilerParams(vmem_limit_bytes=LIMIT),
+        name="merge",
+    )(core, term, lax.ppermute(away, "core", SWAP))
     shards = [to_rows(value) for value in (master, first_moment, second_moment)]
     packed = local(
         plane_sum, shape((depth + 4,) + tile, bf16), 4, VMEM, (pltpu.VMEM((depth,) + tile, f32),)
-    )(exchange(term, PLANE), *shards)
+    )(exchange(term, PLANE[:2]), *shards)
     column = lax.all_gather(packed, "z")
     grad, piece = local(
         column_sum,
@@ -218,8 +236,7 @@
     fresh = [from_rows(value, taps) for value in advance(scale, grad, *shards)]
     update, new_master, new_first, new_second = fresh
     own = exchange(rows, PLANE[:2])
-    other = lax.ppermute(own, "core", [(0, 1), (1, 0)])
-    core = lax.axis_index("core").reshape(1)
+    other = lax.ppermute(own, "core", SWAP)
     whole = put_half(core, own)
     whole = put_half(1 - core, other, whole)
     new_weights = from_rows(whole, taps)

time: 104 us -> 103 us (level)
  blocking collectives: 70.6 us -> 57.7 us
  starting transfers between devices: 15.2 us -> 25 us
  waiting for transfers between devices: 5.21 us -> 6.73 us
    all_to_all x2, blocking collectives: 39.7 us -> 26 us  [exchange(): return lax.all_to_all(value, axes, 0, 0, tiled=False)]
    ppermute x1 -> x2, starting transfers between devices: 3.98 us -> 12.7 us  [the longest x1 8.75 us: body(): lax.ppermute(away, 'core', SWAP)]
    ppermute x1 -> x2, waiting for transfers between devices: 0.01 us -> 1.52 us  [the longest x1 1.51 us: body(): lax.ppermute(away, 'core', SWAP)]
  transfers between devices with their start and end apart: 2 -> 3, of which waited for: 1 -> 2; matrix products, arithmetic and copies ran while one was open for 3% -> 3% of each run, Pallas kernels for 1% -> 1%
where the time goes in v8:
time: 103 us; the launch traced here: 102 us
  blocking collectives  57.7 us (56%)
  starting transfers between devices  25 us (24%)
  waiting for transfers between devices  6.73 us (7%)
  Pallas kernels  4.71 us (5%)
  local copies, waits for them, and re-layouts  4.53 us (4%)
  matrix products  2.09 us (2%)
    all_gather x1, blocking collectives, body(): column = lax.all_gather(packed, 'z')  31.6 us
    all_to_all x2, blocking collectives, exchange(): return lax.all_to_all(value, axes, 0, 0, tiled=False)  26 us
    all_to_all x1, starting transfers between devices, exchange(): return lax.all_to_all(value, axes, 0, 0, tiled=False)  12.3 us
    ppermute x1, starting transfers between devices, body(): lax.ppermute(away, 'core', SWAP)  8.75 us
    all_to_all x1, waiting for transfers between devices, exchange(): return lax.all_to_all(value, axes, 0, 0, tiled=False)  5.21 us
    ppermute x1, starting transfers between devices, body(): other = lax.ppermute(own, 'core', SWAP)  3.98 us
  transfers between devices with their start and end apart: 3, of which 2 were waited for; matrix products, arithmetic and copies ran while one was open for 3% of the time, Pallas kernels for 1%

profile of v8, /device:TPU:1, one launch (start us, length us, event | category | flops | bytes accessed | tf_op | source)
XLA Modules:
  0.0 102.2 jit_solution(3879674094371711528)
XLA Ops:
  0.6 1.5 %slice.3 = bf16[4,198,512]{2,0,1:T(4,128)(2,1)S(1)} slice(bf16[4,199,512]{2,0,1:T(4,128)(2,1)} %param.9), slice={[0:4], [0:198], [0:512]} | slice | bytes 1622016 | tf_op jit(solution)/shard_map/slice | solution.py:61
  2.2 0.0 copy-start
  2.2 0.0 copy-start.1
  2.2 0.0 copy-start.5
  2.2 0.0 copy-start.6
  2.2 0.7 convolution_bitcast_fusion.pre
  2.9 0.5 copy-done
  3.4 1.6 %middle.1 = bf16[4,99,512]{2,1,0:T(8,128)(2,1)S(1)} custom-call(f32[4,99,512]{2,1,0:T(8,128)S(1)} %convolution_bitcast_fusion.pre, f32[1,512]{1,0:T(1,128)S(1)} %bitcast.94, f32[1,512]{1,0:T(1,128)S(1)} %bitcast.95, bf16[512,1024]{1,0:T(8,128)(2,1)S(1)} %copy-done, f32[4,1024]{1,0:T(4,128)S(1)} %copy-done.1), custom_call_target="tpu_custom_call" | custom-call | tf_op jit(solution)/shard_map/middle/pallas_call | solution.py:64
  5.0 0.8 bitcast_convert_fusion
  5.9 0.6 copy.67
  6.5 8.7 %collective-permute-start = (bf16[16,2,16,512]{3,2,1,0:T(8,128)(2,1)S(1)}, bf16[16,2,16,512]{3,2,1,0:T(8,128)(2,1)S(1)}, u32[]{:S(2)}, u32[]{:S(2)}) collective-permute-start(bf16[16,2,16,512]{3,2,1,0:T(8,128)(2,1)S(1)} %dynamic-slice_bitcast_fusion), channel_id=1, source_target_pairs={{0,1},{1,0},{2,3},{3,2},{4,5},{5,4},{6,7},{7,6},{8,9},{9,8},{10,11... | collective-permute-start | bytes 1572872 | tf_op jit(solution)/shard_map/ppermute | solution.py:216
  15.3 1.5 %collective-permute-done.recv = bf16[16,2,16,512]{3,2,1,0:T(8,128)(2,1)S(1)} collective-permute-done((bf16[16,2,16,512]{3,2,1,0:T(8,128)(2,1)S(1)}, bf16[16,2,16,512]{3,2,1,0:T(8,128)(2,1)S(1)}, u32[]{:S(2)}, u32[]{:S(2)}) %collective-permute-start) | collective-permute-done | bytes 524320 | tf_op jit(solution)/shard_map/ppermute | solution.py:216
  16.8 0.1 merge.1
  16.9 0.0 copy-start.2
  16.9 0.0 copy-start.3
  16.9 0.0 copy-start.4
  16.9 12.9 %all_to_all.15.recv = bf16[16,2,16,512]{3,2,1,0:T(8,128)(2,1)S(1)} all-to-all(bf16[16,2,16,512]{3,2,1,0:T(8,128)(2,1)S(1)} %merge.1), channel_id=1, replica_groups=mesh['z'=16,'x'=4,'y'=4,'core'=2] {'x','y'}, dimensions={0} | all-to-all | bytes 1048576 | tf_op jit(solution)/shard_map/all_to_all | solution.py:183
  29.9 0.1 plane_sum.1
  30.0 31.6 %all-gather = bf16[320,8,128]{2,1,0:T(8,128)(2,1)S(1)} all-gather(bf16[20,8,128]{2,1,0:T(8,128)(2,1)S(1)} %plane_sum.1), channel_id=2, replica_groups=mesh['z'=16,'x'=4,'y'=4,'core'=2] {'z'}, dimensions={0}, use_global_device_ids=true | all-gather | bytes 696320 | tf_op jit(solution)/shard_map/all_gather | solution.py:221
  61.7 0.8 column_sum.1
  62.5 12.3 %all-to-all-start.1 = ((f32[32,8,128]{2,1,0:T(8,128)}), f32[32,8,128]{2,1,0:T(8,128)S(1)}, u32[]{:S(2)}, u32[]{:S(2)}) async-start(f32[32,8,128]{2,1,0:T(8,128)} %get-tuple-element.12), calls=%async_computation.1 | async-start | bytes 262144 | tf_op jit(solution)/shard_map/all_to_all | solution.py:183
  74.8 0.6 convolution_convert_fusion
  75.4 0.6 copy.44
  76.0 1.2 %concatenate.3 = bf16[4,199,512]{2,0,1:T(4,128)(2,1)} pad(bf16[4,198,512]{2,0,1:T(4,128)(2,1)S(1)} %bitcast.97, bf16[]{:T(256)} %constant.12.clone.1), padding=0_0x0_1x0_0 | pad | bytes 1626114 | tf_op jit(solution)/shard_map/concatenate | solution.py:80
  77.2 5.2 %all-to-all-done.1.pieces = f32[32,8,128]{2,1,0:T(8,128)S(1)} async-done(((f32[32,8,128]{2,1,0:T(8,128)}), f32[32,8,128]{2,1,0:T(8,128)S(1)}, u32[]{:S(2)}, u32[]{:S(2)}) %all-to-all-start.1) | async-done | bytes 131104 | tf_op jit(solution)/shard_map/all_to_all | solution.py:183
  82.4 0.2 plane_update.1
  82.6 13.1 %all_to_all.16.source = bf16[16,16,8,128]{3,2,1,0:T(8,128)(2,1)S(1)} all-to-all(bf16[16,16,8,128]{3,2,1,0:T(8,128)(2,1)S(1)} %get-tuple-element.17), channel_id=1, replica_groups=mesh['z'=16,'x'=4,'y'=4,'core'=2] {'x','y'}, dimensions={0} | all-to-all | bytes 1048576 | tf_op jit(solution)/shard_map/all_to_all | solution.py:183
  95.7 4.0 %collective-permute-start.1 = (bf16[16,16,8,128]{3,2,1,0:T(8,128)(2,1)S(1)}, bf16[16,16,8,128]{3,2,1,0:T(8,128)(2,1)S(1)}, u32[]{:S(2)}, u32[]{:S(2)}) collective-permute-start(bf16[16,16,8,128]{3,2,1,0:T(8,128)(2,1)S(1)} %all_to_all.16.source), channel_id=1, source_target_pairs={{0,1},{1,0},{2,3},{3,2},{4,5},{5,4},{6,7},{7,6},{8,9},{9,8},{10,11... | collective-permute-start | bytes 1572872 | tf_op jit(solution)/shard_map/ppermute | solution.py:239
  99.7 0.6 multiply_subtract_fusion
  100.3 0.9 put_half.2.refs_0_
  101.2 0.0 collective-permute-done.1.source
  101.2 0.9 put_half.3
  (9 shorter events, 0.1 us)
Async XLA Ops:
  0.6 1.5 %copy-start.7 = (bf16[2,262144]{1,0:T(2,128)(2,1)S(1)}, bf16[2,262144]{1,0:T(2,128)(2,1)}, u32[]{:S(2)}) copy-start(bf16[2,262144]{1,0:T(2,128)(2,1)} %param.10) | copy-start | bytes 3145732
  2.2 1.2 %copy-start = (bf16[512,1024]{1,0:T(8,128)(2,1)S(1)}, bf16[512,1024]{1,0:T(8,128)(2,1)}, u32[]{:S(2)}) copy-start(bf16[512,1024]{1,0:T(8,128)(2,1)} %projection.1) | copy-start | bytes 3145732
  2.2 1.2 %copy-start.1 = (f32[4,1024]{1,0:T(4,128)S(1)}, f32[4,1024]{1,0:T(4,128)}, u32[]{:S(2)}) copy-start(f32[4,1024]{1,0:T(4,128)} %targets.1) | copy-start | bytes 49156
  2.2 1.2 %copy-start.5 = (f32[512]{0:T(512)S(1)}, f32[512]{0:T(512)}, u32[]{:S(2)}) copy-start(f32[512]{0:T(512)} %param.11) | copy-start | bytes 6148
  2.2 1.2 %copy-start.6 = (f32[512]{0:T(512)S(1)}, f32[512]{0:T(512)}, u32[]{:S(2)}) copy-start(f32[512]{0:T(512)} %param.12) | copy-start | bytes 6148
  6.5 10.3 %collective-permute-start = (bf16[16,2,16,512]{3,2,1,0:T(8,128)(2,1)S(1)}, bf16[16,2,16,512]{3,2,1,0:T(8,128)(2,1)S(1)}, u32[]{:S(2)}, u32[]{:S(2)}) collective-permute-start(bf16[16,2,16,512]{3,2,1,0:T(8,128)(2,1)S(1)} %dynamic-slice_bitcast_fusion), channel_id=1, source_target_pairs={{0,1},{1,0},{2,3},{3,2},{4,5},{5,4},{6,7},{7,6},{8,9},{9,8},{10,11... | collective-permute-start | bytes 1572872 | tf_op jit(solution)/shard_map/ppermute | solution.py:216
  16.9 13.0 %copy-start.2 = (f32[2,512]{1,0:T(2,128)S(1)}, f32[2,512]{1,0:T(2,128)}, u32[]{:S(2)}) copy-start(f32[2,512]{1,0:T(2,128)} %param.15) | copy-start | bytes 12292
  16.9 13.0 %copy-start.3 = (f32[2,512]{1,0:T(2,128)S(1)}, f32[2,512]{1,0:T(2,128)}, u32[]{:S(2)}) copy-start(f32[2,512]{1,0:T(2,128)} %param.16) | copy-start | bytes 12292
  16.9 13.0 %copy-start.4 = (f32[2,512]{1,0:T(2,128)S(1)}, f32[2,512]{1,0:T(2,128)}, u32[]{:S(2)}) copy-start(f32[2,512]{1,0:T(2,128)} %param.17) | copy-start | bytes 12292
  62.5 19.9 %all-to-all-start.1 = ((f32[32,8,128]{2,1,0:T(8,128)}), f32[32,8,128]{2,1,0:T(8,128)S(1)}, u32[]{:S(2)}, u32[]{:S(2)}) async-start(f32[32,8,128]{2,1,0:T(8,128)} %get-tuple-element.12), calls=%async_computation.1 | async-start | bytes 262144 | tf_op jit(solution)/shard_map/all_to_all | solution.py:183
  95.7 5.5 %collective-permute-start.1 = (bf16[16,16,8,128]{3,2,1,0:T(8,128)(2,1)S(1)}, bf16[16,16,8,128]{3,2,1,0:T(8,128)(2,1)S(1)}, u32[]{:S(2)}, u32[]{:S(2)}) collective-permute-start(bf16[16,16,8,128]{3,2,1,0:T(8,128)(2,1)S(1)} %all_to_all.16.source), channel_id=1, source_target_pairs={{0,1},{1,0},{2,3},{3,2},{4,5},{5,4},{6,7},{7,6},{8,9},{9,8},{10,11... | collective-permute-start | bytes 1572872 | tf_op jit(solution)/shard_map/ppermute | solution.py:239

commit v9 on v8

--- a/solution.py
+++ b/solution.py
@@ -206,6 +206,8 @@
     term = lax.optimization_barrier(term).reshape(plane // 2, 2, taps, depth, width)
     core = lax.axis_index("core").reshape(1)
     away = lax.dynamic_index_in_dim(term, 1 - core[0], 1, keepdims=False)
+    recv = lax.ppermute(away, "core", SWAP)
+    recv, input_grad = lax.optimization_barrier((recv, input_grad))
     term = pl.pallas_call(
         merge,
         out_shape=shape(away.shape, bf16),
@@ -213,7 +215,7 @@
         out_specs=VMEM,
         compiler_params=pltpu.CompilerParams(vmem_limit_bytes=LIMIT),
         name="merge",
-    )(core, term, lax.ppermute(away, "core", SWAP))
+    )(core, term, recv)
     shards = [to_rows(value) for value in (master, first_moment, second_moment)]
     packed = local(
         plane_sum, shape((depth + 4,) + tile, bf16), 4, VMEM, (pltpu.VMEM((depth,) + tile, f32),)
@@ -225,13 +227,12 @@
         1,
         (VMEM, VMEM),
     )(column)
-    pieces, input_grad = lax.optimization_barrier((exchange(piece, PLANE), input_grad))
     rows, scale = local(
         plane_update,
         (shape((plane // 2, depth) + tile, bf16), shape((8, LANES), f32)),
         3,
         (VMEM, VMEM),
-    )(pieces, grad, column)
+    )(exchange(piece, PLANE), grad, column)
     grad = lax.dynamic_index_in_dim(grad, lax.axis_index("z"), 0, keepdims=False)
     fresh = [from_rows(value, taps) for value in advance(scale, grad, *shards)]
     update, new_master, new_first, new_second = fresh

time: 103 us -> 102 us (level)
  blocking collectives: 57.7 us -> 77.1 us
  starting transfers between devices: 25 us -> 12.7 us
  waiting for transfers between devices: 6.73 us -> 0.01 us
    all_to_all x2 -> x3, blocking collectives: 26 us -> 46.5 us  [exchange(): return lax.all_to_all(value, axes, 0, 0, tiled=False)]
    all_to_all x1 -> x0, starting transfers between devices: 12.3 us -> none  [exchange(): return lax.all_to_all(value, axes, 0, 0, tiled=False)]
    all_to_all x1 -> x0, waiting for transfers between devices: 5.21 us -> none  [exchange(): return lax.all_to_all(value, axes, 0, 0, tiled=False)]
    ppermute x1, waiting for transfers between devices: 1.51 us -> 0.01 us  [body(): recv = lax.ppermute(away, 'core', SWAP)]
    all_gather x1, blocking collectives: 31.6 us -> 30.6 us  [body(): column = lax.all_gather(packed, 'z')]
  transfers between devices with their start and end apart: 3 -> 2, of which waited for: 2 -> 0; matrix products, arithmetic and copies ran while one was open for 3% -> 3% of each run, Pallas kernels for 1% -> 1%
where the time goes in v9:
time: 102 us
  blocking collectives  77.1 us (76%)
  starting transfers between devices  12.7 us (12%)
  local copies, waits for them, and re-layouts  4.53 us (4%)
  Pallas kernels  4.04 us (4%)
  matrix products  2.09 us (2%)
    all_to_all x3, blocking collectives, exchange(): return lax.all_to_all(value, axes, 0, 0, tiled=False)  46.5 us
    all_gather x1, blocking collectives, body(): column = lax.all_gather(packed, 'z')  30.6 us
    ppermute x1, starting transfers between devices, body(): recv = lax.ppermute(away, 'core', SWAP)  8.75 us
    ppermute x1, starting transfers between devices, body(): other = lax.ppermute(own, 'core', SWAP)  3.98 us
  transfers between devices with their start and end apart: 2, of which 0 were waited for; matrix products, arithmetic and copies ran while one was open for 3% of the time, Pallas kernels for 1%

profile of v9, /device:TPU:1, one launch (start us, length us, event | category | flops | bytes accessed | tf_op | source)
XLA Modules:
  0.0 101.9 jit_solution(6885255245017922970)
XLA Ops:
  0.6 1.5 %slice.3 = bf16[4,198,512]{2,0,1:T(4,128)(2,1)S(1)} slice(bf16[4,199,512]{2,0,1:T(4,128)(2,1)} %param.9), slice={[0:4], [0:198], [0:512]} | slice | bytes 1622016 | tf_op jit(solution)/shard_map/slice | solution.py:61
  2.2 0.0 copy-start
  2.2 0.0 copy-start.1
  2.2 0.0 copy-start.5
  2.2 0.0 copy-start.6
  2.2 0.7 convolution_bitcast_fusion.pre
  2.9 0.5 copy-done
  3.4 0.0 copy-done.5
  3.4 1.6 %middle.1 = bf16[4,99,512]{2,1,0:T(8,128)(2,1)S(1)} custom-call(f32[4,99,512]{2,1,0:T(8,128)S(1)} %convolution_bitcast_fusion.pre, f32[1,512]{1,0:T(1,128)S(1)} %bitcast.94, f32[1,512]{1,0:T(1,128)S(1)} %bitcast.95, bf16[512,1024]{1,0:T(8,128)(2,1)S(1)} %copy-done, f32[4,1024]{1,0:T(4,128)S(1)} %copy-done.1), custom_call_target="tpu_custom_call" | custom-call | tf_op jit(solution)/shard_map/middle/pallas_call | solution.py:64
  5.0 0.8 bitcast_convert_fusion
  5.9 0.6 copy.67
  6.5 8.7 %collective-permute-start = (bf16[16,2,16,512]{3,2,1,0:T(8,128)(2,1)S(1)}, bf16[16,2,16,512]{3,2,1,0:T(8,128)(2,1)S(1)}, u32[]{:S(2)}, u32[]{:S(2)}) collective-permute-start(bf16[16,2,16,512]{3,2,1,0:T(8,128)(2,1)S(1)} %dynamic-slice_bitcast_fusion), channel_id=1, source_target_pairs={{0,1},{1,0},{2,3},{3,2},{4,5},{5,4},{6,7},{7,6},{8,9},{9,8},{10,11... | collective-permute-start | bytes 1572872 | tf_op jit(solution)/shard_map/ppermute | solution.py:209
  15.3 0.6 convolution_convert_fusion
  15.9 0.6 copy.41
  16.5 1.2 %concatenate.3 = bf16[4,199,512]{2,0,1:T(4,128)(2,1)} pad(bf16[4,198,512]{2,0,1:T(4,128)(2,1)S(1)} %bitcast.97, bf16[]{:T(256)} %constant.12.clone.1), padding=0_0x0_1x0_0 | pad | bytes 1626114 | tf_op jit(solution)/shard_map/concatenate | solution.py:80
  17.7 0.0 collective-permute-done.recv
  17.7 0.1 merge.1
  17.8 0.0 copy-start.2
  17.9 0.0 copy-start.3
  17.9 0.0 copy-start.4
  17.9 13.3 %all_to_all.15.recv = bf16[16,2,16,512]{3,2,1,0:T(8,128)(2,1)S(1)} all-to-all(bf16[16,2,16,512]{3,2,1,0:T(8,128)(2,1)S(1)} %merge.1), channel_id=1, replica_groups=mesh['z'=16,'x'=4,'y'=4,'core'=2] {'x','y'}, dimensions={0} | all-to-all | bytes 1048576 | tf_op jit(solution)/shard_map/all_to_all | solution.py:183
  31.2 0.1 plane_sum.1
  31.4 30.6 %all-gather = bf16[320,8,128]{2,1,0:T(8,128)(2,1)S(1)} all-gather(bf16[20,8,128]{2,1,0:T(8,128)(2,1)S(1)} %plane_sum.1), channel_id=2, replica_groups=mesh['z'=16,'x'=4,'y'=4,'core'=2] {'z'}, dimensions={0}, use_global_device_ids=true | all-gather | bytes 696320 | tf_op jit(solution)/shard_map/all_gather | solution.py:223
  61.9 0.2 column_sum.1
  62.1 20.1 %all_to_all.16.pieces = f32[32,8,128]{2,1,0:T(8,128)S(1)} all-to-all(f32[32,8,128]{2,1,0:T(8,128)S(1)} %get-tuple-element.14), channel_id=1, replica_groups=mesh['z'=16,'x'=4,'y'=4,'core'=2] {'x','y','core'}, dimensions={0} | all-to-all | bytes 262144 | tf_op jit(solution)/shard_map/all_to_all | solution.py:183
  82.2 0.2 plane_update.1
  82.4 13.1 %all_to_all.17.source = bf16[16,16,8,128]{3,2,1,0:T(8,128)(2,1)S(1)} all-to-all(bf16[16,16,8,128]{3,2,1,0:T(8,128)(2,1)S(1)} %get-tuple-element.17), channel_id=1, replica_groups=mesh['z'=16,'x'=4,'y'=4,'core'=2] {'x','y'}, dimensions={0} | all-to-all | bytes 1048576 | tf_op jit(solution)/shard_map/all_to_all | solution.py:183
  95.5 4.0 %collective-permute-start.1 = (bf16[16,16,8,128]{3,2,1,0:T(8,128)(2,1)S(1)}, bf16[16,16,8,128]{3,2,1,0:T(8,128)(2,1)S(1)}, u32[]{:S(2)}, u32[]{:S(2)}) collective-permute-start(bf16[16,16,8,128]{3,2,1,0:T(8,128)(2,1)S(1)} %all_to_all.17.source), channel_id=1, source_target_pairs={{0,1},{1,0},{2,3},{3,2},{4,5},{5,4},{6,7},{7,6},{8,9},{9,8},{10,11... | collective-permute-start | bytes 1572872 | tf_op jit(solution)/shard_map/ppermute | solution.py:240
  99.5 0.6 multiply_subtract_fusion
  100.1 0.9 put_half.2.refs_0_
  101.0 0.0 collective-permute-done.1.source
  101.0 0.9 put_half.3
  (8 shorter events, 0.1 us)
Async XLA Ops:
  0.6 1.5 %copy-start.7 = (bf16[2,262144]{1,0:T(2,128)(2,1)S(1)}, bf16[2,262144]{1,0:T(2,128)(2,1)}, u32[]{:S(2)}) copy-start(bf16[2,262144]{1,0:T(2,128)(2,1)} %param.10) | copy-start | bytes 3145732
  2.2 1.2 %copy-start = (bf16[512,1024]{1,0:T(8,128)(2,1)S(1)}, bf16[512,1024]{1,0:T(8,128)(2,1)}, u32[]{:S(2)}) copy-start(bf16[512,1024]{1,0:T(8,128)(2,1)} %projection.1) | copy-start | bytes 3145732
  2.2 1.2 %copy-start.1 = (f32[4,1024]{1,0:T(4,128)S(1)}, f32[4,1024]{1,0:T(4,128)}, u32[]{:S(2)}) copy-start(f32[4,1024]{1,0:T(4,128)} %targets.1) | copy-start | bytes 49156
  2.2 1.2 %copy-start.5 = (f32[512]{0:T(512)S(1)}, f32[512]{0:T(512)}, u32[]{:S(2)}) copy-start(f32[512]{0:T(512)} %param.11) | copy-start | bytes 6148
  2.2 1.2 %copy-start.6 = (f32[512]{0:T(512)S(1)}, f32[512]{0:T(512)}, u32[]{:S(2)}) copy-start(f32[512]{0:T(512)} %param.12) | copy-start | bytes 6148
  6.5 11.2 %collective-permute-start = (bf16[16,2,16,512]{3,2,1,0:T(8,128)(2,1)S(1)}, bf16[16,2,16,512]{3,2,1,0:T(8,128)(2,1)S(1)}, u32[]{:S(2)}, u32[]{:S(2)}) collective-permute-start(bf16[16,2,16,512]{3,2,1,0:T(8,128)(2,1)S(1)} %dynamic-slice_bitcast_fusion), channel_id=1, source_target_pairs={{0,1},{1,0},{2,3},{3,2},{4,5},{5,4},{6,7},{7,6},{8,9},{9,8},{10,11... | collective-permute-start | bytes 1572872 | tf_op jit(solution)/shard_map/ppermute | solution.py:209
  17.8 13.4 %copy-start.2 = (f32[2,512]{1,0:T(2,128)S(1)}, f32[2,512]{1,0:T(2,128)}, u32[]{:S(2)}) copy-start(f32[2,512]{1,0:T(2,128)} %param.15) | copy-start | bytes 12292
  17.9 13.4 %copy-start.3 = (f32[2,512]{1,0:T(2,128)S(1)}, f32[2,512]{1,0:T(2,128)}, u32[]{:S(2)}) copy-start(f32[2,512]{1,0:T(2,128)} %param.16) | copy-start | bytes 12292
  17.9 13.4 %copy-start.4 = (f32[2,512]{1,0:T(2,128)S(1)}, f32[2,512]{1,0:T(2,128)}, u32[]{:S(2)}) copy-start(f32[2,512]{1,0:T(2,128)} %param.17) | copy-start | bytes 12292
  95.5 5.5 %collective-permute-start.1 = (bf16[16,16,8,128]{3,2,1,0:T(8,128)(2,1)S(1)}, bf16[16,16,8,128]{3,2,1,0:T(8,128)(2,1)S(1)}, u32[]{:S(2)}, u32[]{:S(2)}) collective-permute-start(bf16[16,16,8,128]{3,2,1,0:T(8,128)(2,1)S(1)} %all_to_all.17.source), channel_id=1, source_target_pairs={{0,1},{1,0},{2,3},{3,2},{4,5},{5,4},{6,7},{7,6},{8,9},{9,8},{10,11... | collective-permute-start | bytes 1572872 | tf_op jit(solution)/shard_map/ppermute | solution.py:240

commit v10 on v9

--- a/solution.py
+++ b/solution.py
@@ -21,7 +21,7 @@
     return [slice(start, min(start + 8, frames)) for start in range(0, frames, 8)]
 
 
-def middle(pre, gain, bias, projection, targets, dpre, normed, slope, deviation):
+def forward(pre, gain, bias, normed, slope, deviation, pool):
     clips, frames, width = pre.shape
     gains, biases = gain[...][None], bias[...][None]
     pooled = jnp.zeros((clips, width), jnp.float32)
@@ -38,8 +38,12 @@
         normed[:, rows, :] = normal
         slope[:, rows, :] = (share + point * bell) * gains
         deviation[:, rows, :] = jnp.broadcast_to(inverse, inverse.shape[:2] + (LANES,))
-    pooled = (pooled / frames).astype(jnp.bfloat16)
-    predicted = jnp.dot(pooled, projection[...], preferred_element_type=jnp.float32)
+    pool[...] = (pooled / frames).astype(jnp.bfloat16)
+
+
+def backward(normed, slope, deviation, pool, projection, targets, dpre):
+    frames = dpre.shape[1]
+    predicted = jnp.dot(pool[...], projection[...], preferred_element_type=jnp.float32)
     miss = (predicted - targets[...]).astype(jnp.bfloat16)
     back = lax.dot_general(
         miss, projection[...], (((1,), (1,)), ((), ())), preferred_element_type=jnp.float32
@@ -61,17 +65,19 @@
     windows = inputs[:, : frames_out * taps].reshape(clips, frames_out, taps, chans)
     kernel = weights.reshape(taps, chans, chans)
     pre = jnp.einsum("bfki,koi->bfo", windows, kernel, preferred_element_type=jnp.float32)
-    dpre = local(
-        middle,
-        jax.ShapeDtypeStruct(pre.shape, jnp.bfloat16),
-        5,
-        VMEM,
+    shape, f32, bf16 = jax.ShapeDtypeStruct, jnp.float32, jnp.bfloat16
+    saved = local(
+        forward,
         (
-            pltpu.VMEM(pre.shape, jnp.float32),
-            pltpu.VMEM(pre.shape, jnp.float32),
-            pltpu.VMEM(pre.shape[:2] + (LANES,), jnp.float32),
+            shape(pre.shape, f32),
+            shape(pre.shape, f32),
+            shape(pre.shape[:2] + (LANES,), f32),
+            shape((clips, chans), bf16),
         ),
-    )(pre, ln_gain[None], ln_bias[None], projection, targets)
+        3,
+        (VMEM,) * 4,
+    )(pre, ln_gain[None], ln_bias[None])
+    dpre = local(backward, shape(pre.shape, bf16), 6)(*saved, projection, targets)
     dwin = jnp.einsum("bfo,koi->bfki", dpre, kernel, preferred_element_type=jnp.float32).astype(
         jnp.bfloat16
     )

time: 102 us -> 102 us (level)
  no operation moved by 1% of the time
where the time goes in v10:
time: 102 us
  blocking collectives  77.1 us (76%)
  starting transfers between devices  12.7 us (12%)
  Pallas kernels  4.13 us (4%)
  local copies, waits for them, and re-layouts  4.02 us (4%)
  matrix products  2.09 us (2%)
    all_to_all x3, blocking collectives, exchange(): return lax.all_to_all(value, axes, 0, 0, tiled=False)  46.6 us
    all_gather x1, blocking collectives, body(): column = lax.all_gather(packed, 'z')  30.6 us
    ppermute x1, starting transfers between devices, body(): recv = lax.ppermute(away, 'core', SWAP)  8.75 us
    ppermute x1, starting transfers between devices, body(): other = lax.ppermute(own, 'core', SWAP)  3.98 us
  transfers between devices with their start and end apart: 2, of which 0 were waited for; matrix products, arithmetic and copies ran while one was open for 3% of the time, Pallas kernels for 1%

profile of v10, /device:TPU:1, one launch (start us, length us, event | category | flops | bytes accessed | tf_op | source)
XLA Modules:
  0.0 101.6 jit_solution(869595909656319958)
XLA Ops:
  0.6 0.0 copy-start.7
  0.6 1.5 %slice.3 = bf16[4,198,512]{2,0,1:T(4,128)(2,1)S(1)} slice(bf16[4,199,512]{2,0,1:T(4,128)(2,1)} %param.9), slice={[0:4], [0:198], [0:512]} | slice | bytes 1622016 | tf_op jit(solution)/shard_map/slice | solution.py:65
  2.2 0.0 copy-start.5
  2.2 0.0 copy-start.6
  2.2 0.0 copy-start
  2.2 0.0 copy-start.4
  2.2 0.7 convolution_bitcast_fusion.pre
  2.9 0.9 forward.1
  3.8 0.8 backward.1
  4.6 0.8 bitcast_convert_fusion
  5.5 0.6 copy.67
  6.1 8.8 %collective-permute-start = (bf16[16,2,16,512]{3,2,1,0:T(8,128)(2,1)S(1)}, bf16[16,2,16,512]{3,2,1,0:T(8,128)(2,1)S(1)}, u32[]{:S(2)}, u32[]{:S(2)}) collective-permute-start(bf16[16,2,16,512]{3,2,1,0:T(8,128)(2,1)S(1)} %dynamic-slice_bitcast_fusion), channel_id=1, source_target_pairs={{0,1},{1,0},{2,3},{3,2},{4,5},{5,4},{6,7},{7,6},{8,9},{9,8},{10,11... | collective-permute-start | bytes 1572872 | tf_op jit(solution)/shard_map/ppermute | solution.py:215
  14.9 0.6 convolution_convert_fusion
  15.5 0.6 copy.41
  16.1 1.2 %concatenate.3 = bf16[4,199,512]{2,0,1:T(4,128)(2,1)} pad(bf16[4,198,512]{2,0,1:T(4,128)(2,1)S(1)} %bitcast.97, bf16[]{:T(256)} %constant.12.clone.1), padding=0_0x0_1x0_0 | pad | bytes 1626114 | tf_op jit(solution)/shard_map/concatenate | solution.py:86
  17.3 0.0 collective-permute-done.recv
  17.3 0.1 merge.1
  17.5 0.0 copy-start.1
  17.5 0.0 copy-start.2
  17.5 0.0 copy-start.3
  17.5 13.3 %all_to_all.15.recv = bf16[16,2,16,512]{3,2,1,0:T(8,128)(2,1)S(1)} all-to-all(bf16[16,2,16,512]{3,2,1,0:T(8,128)(2,1)S(1)} %merge.1), channel_id=1, replica_groups=mesh['z'=16,'x'=4,'y'=4,'core'=2] {'x','y'}, dimensions={0} | all-to-all | bytes 1048576 | tf_op jit(solution)/shard_map/all_to_all | solution.py:189
  30.9 0.1 plane_sum.1
  31.0 30.6 %all-gather = bf16[320,8,128]{2,1,0:T(8,128)(2,1)S(1)} all-gather(bf16[20,8,128]{2,1,0:T(8,128)(2,1)S(1)} %plane_sum.1), channel_id=2, replica_groups=mesh['z'=16,'x'=4,'y'=4,'core'=2] {'z'}, dimensions={0}, use_global_device_ids=true | all-gather | bytes 696320 | tf_op jit(solution)/shard_map/all_gather | solution.py:229
  61.5 0.2 column_sum.1
  61.7 20.1 %all_to_all.16.pieces = f32[32,8,128]{2,1,0:T(8,128)S(1)} all-to-all(f32[32,8,128]{2,1,0:T(8,128)S(1)} %get-tuple-element.22), channel_id=1, replica_groups=mesh['z'=16,'x'=4,'y'=4,'core'=2] {'x','y','core'}, dimensions={0} | all-to-all | bytes 262144 | tf_op jit(solution)/shard_map/all_to_all | solution.py:189
  81.9 0.2 plane_update.1
  82.0 13.1 %all_to_all.17.source = bf16[16,16,8,128]{3,2,1,0:T(8,128)(2,1)S(1)} all-to-all(bf16[16,16,8,128]{3,2,1,0:T(8,128)(2,1)S(1)} %get-tuple-element.25), channel_id=1, replica_groups=mesh['z'=16,'x'=4,'y'=4,'core'=2] {'x','y'}, dimensions={0} | all-to-all | bytes 1048576 | tf_op jit(solution)/shard_map/all_to_all | solution.py:189
  95.1 4.0 %collective-permute-start.1 = (bf16[16,16,8,128]{3,2,1,0:T(8,128)(2,1)S(1)}, bf16[16,16,8,128]{3,2,1,0:T(8,128)(2,1)S(1)}, u32[]{:S(2)}, u32[]{:S(2)}) collective-permute-start(bf16[16,16,8,128]{3,2,1,0:T(8,128)(2,1)S(1)} %all_to_all.17.source), channel_id=1, source_target_pairs={{0,1},{1,0},{2,3},{3,2},{4,5},{5,4},{6,7},{7,6},{8,9},{9,8},{10,11... | collective-permute-start | bytes 1572872 | tf_op jit(solution)/shard_map/ppermute | solution.py:246
  99.1 0.6 multiply_subtract_fusion
  99.7 0.9 put_half.2.refs_0_
  100.6 0.0 collective-permute-done.1.source
  100.6 0.9 put_half.3
  (9 shorter events, 0.1 us)
Async XLA Ops:
  0.6 1.5 %copy-start.7 = (bf16[2,262144]{1,0:T(2,128)(2,1)S(1)}, bf16[2,262144]{1,0:T(2,128)(2,1)}, u32[]{:S(2)}) copy-start(bf16[2,262144]{1,0:T(2,128)(2,1)} %param.10) | copy-start | bytes 3145732
  2.2 0.7 copy-start.5
  2.2 0.7 copy-start.6
  2.2 1.6 %copy-start = (bf16[512,1024]{1,0:T(8,128)(2,1)S(1)}, bf16[512,1024]{1,0:T(8,128)(2,1)}, u32[]{:S(2)}) copy-start(bf16[512,1024]{1,0:T(8,128)(2,1)} %projection.1) | copy-start | bytes 3145732
  2.2 1.6 %copy-start.4 = (f32[4,1024]{1,0:T(4,128)S(1)}, f32[4,1024]{1,0:T(4,128)}, u32[]{:S(2)}) copy-start(f32[4,1024]{1,0:T(4,128)} %targets.1) | copy-start | bytes 49156
  6.1 11.2 %collective-permute-start = (bf16[16,2,16,512]{3,2,1,0:T(8,128)(2,1)S(1)}, bf16[16,2,16,512]{3,2,1,0:T(8,128)(2,1)S(1)}, u32[]{:S(2)}, u32[]{:S(2)}) collective-permute-start(bf16[16,2,16,512]{3,2,1,0:T(8,128)(2,1)S(1)} %dynamic-slice_bitcast_fusion), channel_id=1, source_target_pairs={{0,1},{1,0},{2,3},{3,2},{4,5},{5,4},{6,7},{7,6},{8,9},{9,8},{10,11... | collective-permute-start | bytes 1572872 | tf_op jit(solution)/shard_map/ppermute | solution.py:215
  17.5 13.4 %copy-start.1 = (f32[2,512]{1,0:T(2,128)S(1)}, f32[2,512]{1,0:T(2,128)}, u32[]{:S(2)}) copy-start(f32[2,512]{1,0:T(2,128)} %param.15) | copy-start | bytes 12292
  17.5 13.4 %copy-start.2 = (f32[2,512]{1,0:T(2,128)S(1)}, f32[2,512]{1,0:T(2,128)}, u32[]{:S(2)}) copy-start(f32[2,512]{1,0:T(2,128)} %param.16) | copy-start | bytes 12292
  17.5 13.4 %copy-start.3 = (f32[2,512]{1,0:T(2,128)S(1)}, f32[2,512]{1,0:T(2,128)}, u32[]{:S(2)}) copy-start(f32[2,512]{1,0:T(2,128)} %param.17) | copy-start | bytes 12292
  95.1 5.5 %collective-permute-start.1 = (bf16[16,16,8,128]{3,2,1,0:T(8,128)(2,1)S(1)}, bf16[16,16,8,128]{3,2,1,0:T(8,128)(2,1)S(1)}, u32[]{:S(2)}, u32[]{:S(2)}) collective-permute-start(bf16[16,16,8,128]{3,2,1,0:T(8,128)(2,1)S(1)} %all_to_all.17.source), channel_id=1, source_target_pairs={{0,1},{1,0},{2,3},{3,2},{4,5},{5,4},{6,7},{7,6},{8,9},{9,8},{10,11... | collective-permute-start | bytes 1572872 | tf_op jit(solution)/shard_map/ppermute | solution.py:246

commit v11 on v10

--- a/solution.py
+++ b/solution.py
@@ -56,6 +56,17 @@
         second = jnp.mean(grad * normal, axis=-1, keepdims=True)
         inverse = deviation[:, rows, 0:1]
         dpre[:, rows, :] = (inverse * (grad - first - normal * second)).astype(jnp.bfloat16)
+
+
+def with_tail(frames, out, tail, sems):
+    count = frames.shape[0]
+    body_copy = pltpu.make_async_copy(frames, out.at[pl.ds(0, count)], sems.at[0])
+    body_copy.start()
+    tail[...] = jnp.zeros_like(tail)
+    tail_copy = pltpu.make_async_copy(tail, out.at[pl.ds(count, tail.shape[0])], sems.at[1])
+    tail_copy.start()
+    body_copy.wait()
+    tail_copy.wait()
 
 
 def local_pass(inputs, weights, ln_gain, ln_bias, projection, targets):
@@ -81,9 +92,18 @@
     dwin = jnp.einsum("bfo,koi->bfki", dpre, kernel, preferred_element_type=jnp.float32).astype(
         jnp.bfloat16
     )
-    dinput = dwin.reshape(clips, frames_out * taps, chans)
-    tail = jnp.zeros((clips, frames_in - frames_out * taps, chans), jnp.bfloat16)
-    return (windows, dpre, jnp.concatenate([dinput, tail], axis=1))
+    dinput = dwin.reshape(clips, frames_out * taps, chans).transpose(1, 0, 2)
+    rest = frames_in - frames_out * taps
+    dinput = pl.pallas_call(
+        with_tail,
+        out_shape=shape((frames_in, clips, chans), bf16),
+        in_specs=[VMEM],
+        out_specs=pl.BlockSpec(memory_space=pl.ANY),
+        scratch_shapes=[pltpu.VMEM((rest, clips, chans), bf16), pltpu.SemaphoreType.DMA((2,))],
+        compiler_params=pltpu.CompilerParams(vmem_limit_bytes=LIMIT),
+        name="with_tail",
+    )(dinput)
+    return (windows, dpre, dinput.transpose(1, 0, 2))
 
 
 def merge(core, term, recv, out):

time: 102 us -> 102 us (level)
  local copies, waits for them, and re-layouts: 4.02 us -> 2.81 us
    concatenate x1 -> x0, local copies, waits for them, and re-layouts: 1.21 us -> none  [local_pass(): return (windows, dpre, jnp.concatenate([dinput, tail], axis=1))]
  transfers between devices with their start and end apart: 2 -> 2, of which waited for: 0 -> 0; matrix products, arithmetic and copies ran while one was open for 3% -> 2% of each run, Pallas kernels for 1% -> 2%
where the time goes in v11:
time: 102 us; the launch traced here: 101 us
  blocking collectives  77.1 us (76%)
  starting transfers between devices  12.7 us (12%)
  Pallas kernels  5.05 us (5%)
  local copies, waits for them, and re-layouts  2.81 us (3%)
  matrix products  2.09 us (2%)
    all_to_all x3, blocking collectives, exchange(): return lax.all_to_all(value, axes, 0, 0, tiled=False)  46.6 us
    all_gather x1, blocking collectives, body(): column = lax.all_gather(packed, 'z')  30.6 us
    ppermute x1, starting transfers between devices, body(): recv = lax.ppermute(away, 'core', SWAP)  8.75 us
    ppermute x1, starting transfers between devices, body(): other = lax.ppermute(own, 'core', SWAP)  3.98 us
  transfers between devices with their start and end apart: 2, of which 0 were waited for; matrix products, arithmetic and copies ran while one was open for 2% of the time, Pallas kernels for 2%

profile of v11, /device:TPU:1, one launch (start us, length us, event | category | flops | bytes accessed | tf_op | source)
XLA Modules:
  0.0 101.3 jit_solution(12679374964488101963)
XLA Ops:
  0.6 1.5 %slice.3 = bf16[4,198,512]{2,0,1:T(4,128)(2,1)S(1)} slice(bf16[4,199,512]{2,0,1:T(4,128)(2,1)} %param.9), slice={[0:4], [0:198], [0:512]} | slice | bytes 1622016 | tf_op jit(solution)/shard_map/slice | solution.py:76
  2.2 0.0 copy-start.5
  2.2 0.0 copy-start.6
  2.2 0.0 copy-start
  2.2 0.0 copy-start.4
  2.2 0.7 convolution_bitcast_fusion.pre
  2.9 0.9 forward.1
  3.8 0.8 backward.1
  4.6 0.8 bitcast_convert_fusion
  5.5 0.6 copy.68
  6.1 8.8 %collective-permute-start = (bf16[16,2,16,512]{3,2,1,0:T(8,128)(2,1)S(1)}, bf16[16,2,16,512]{3,2,1,0:T(8,128)(2,1)S(1)}, u32[]{:S(2)}, u32[]{:S(2)}) collective-permute-start(bf16[16,2,16,512]{3,2,1,0:T(8,128)(2,1)S(1)} %dynamic-slice_bitcast_fusion), channel_id=1, source_target_pairs={{0,1},{1,0},{2,3},{3,2},{4,5},{5,4},{6,7},{7,6},{8,9},{9,8},{10,11... | collective-permute-start | bytes 1572872 | tf_op jit(solution)/shard_map/ppermute | solution.py:235
  14.9 0.6 convolution_convert_fusion
  15.5 0.6 copy.42
  16.1 0.9 with_tail.1
  17.0 0.0 collective-permute-done.recv
  17.1 0.1 merge.1
  17.2 0.0 copy-start.1
  17.2 0.0 copy-start.2
  17.2 0.0 copy-start.3
  17.2 13.3 %all_to_all.15.recv = bf16[16,2,16,512]{3,2,1,0:T(8,128)(2,1)S(1)} all-to-all(bf16[16,2,16,512]{3,2,1,0:T(8,128)(2,1)S(1)} %merge.1), channel_id=1, replica_groups=mesh['z'=16,'x'=4,'y'=4,'core'=2] {'x','y'}, dimensions={0} | all-to-all | bytes 1048576 | tf_op jit(solution)/shard_map/all_to_all | solution.py:209
  30.6 0.0 copy-done.3
  30.6 0.1 plane_sum.1
  30.7 30.6 %all-gather = bf16[320,8,128]{2,1,0:T(8,128)(2,1)S(1)} all-gather(bf16[20,8,128]{2,1,0:T(8,128)(2,1)S(1)} %plane_sum.1), channel_id=2, replica_groups=mesh['z'=16,'x'=4,'y'=4,'core'=2] {'z'}, dimensions={0}, use_global_device_ids=true | all-gather | bytes 696320 | tf_op jit(solution)/shard_map/all_gather | solution.py:249
  61.3 0.2 column_sum.1
  61.4 20.1 %all_to_all.16.pieces = f32[32,8,128]{2,1,0:T(8,128)S(1)} all-to-all(f32[32,8,128]{2,1,0:T(8,128)S(1)} %get-tuple-element.22), channel_id=1, replica_groups=mesh['z'=16,'x'=4,'y'=4,'core'=2] {'x','y','core'}, dimensions={0} | all-to-all | bytes 262144 | tf_op jit(solution)/shard_map/all_to_all | solution.py:209
  81.6 0.2 plane_update.1
  81.8 13.1 %all_to_all.17.source = bf16[16,16,8,128]{3,2,1,0:T(8,128)(2,1)S(1)} all-to-all(bf16[16,16,8,128]{3,2,1,0:T(8,128)(2,1)S(1)} %get-tuple-element.25), channel_id=1, replica_groups=mesh['z'=16,'x'=4,'y'=4,'core'=2] {'x','y'}, dimensions={0} | all-to-all | bytes 1048576 | tf_op jit(solution)/shard_map/all_to_all | solution.py:209
  94.8 4.0 %collective-permute-start.1 = (bf16[16,16,8,128]{3,2,1,0:T(8,128)(2,1)S(1)}, bf16[16,16,8,128]{3,2,1,0:T(8,128)(2,1)S(1)}, u32[]{:S(2)}, u32[]{:S(2)}) collective-permute-start(bf16[16,16,8,128]{3,2,1,0:T(8,128)(2,1)S(1)} %all_to_all.17.source), channel_id=1, source_target_pairs={{0,1},{1,0},{2,3},{3,2},{4,5},{5,4},{6,7},{7,6},{8,9},{9,8},{10,11... | collective-permute-start | bytes 1572872 | tf_op jit(solution)/shard_map/ppermute | solution.py:266
  98.8 0.6 multiply_subtract_fusion
  99.4 0.9 put_half.2.refs_0_
  100.4 0.0 collective-permute-done.1.source
  100.4 0.9 put_half.3
  (9 shorter events, 0.1 us)
Async XLA Ops:
  0.6 1.5 %copy-start.7 = (bf16[2,262144]{1,0:T(2,128)(2,1)S(1)}, bf16[2,262144]{1,0:T(2,128)(2,1)}, u32[]{:S(2)}) copy-start(bf16[2,262144]{1,0:T(2,128)(2,1)} %param.10) | copy-start | bytes 3145732
  2.2 0.7 copy-start.5
  2.2 0.7 copy-start.6
  2.2 1.6 %copy-start = (bf16[512,1024]{1,0:T(8,128)(2,1)S(1)}, bf16[512,1024]{1,0:T(8,128)(2,1)}, u32[]{:S(2)}) copy-start(bf16[512,1024]{1,0:T(8,128)(2,1)} %projection.1) | copy-start | bytes 3145732
  2.2 1.6 %copy-start.4 = (f32[4,1024]{1,0:T(4,128)S(1)}, f32[4,1024]{1,0:T(4,128)}, u32[]{:S(2)}) copy-start(f32[4,1024]{1,0:T(4,128)} %targets.1) | copy-start | bytes 49156
  6.1 10.9 %collective-permute-start = (bf16[16,2,16,512]{3,2,1,0:T(8,128)(2,1)S(1)}, bf16[16,2,16,512]{3,2,1,0:T(8,128)(2,1)S(1)}, u32[]{:S(2)}, u32[]{:S(2)}) collective-permute-start(bf16[16,2,16,512]{3,2,1,0:T(8,128)(2,1)S(1)} %dynamic-slice_bitcast_fusion), channel_id=1, source_target_pairs={{0,1},{1,0},{2,3},{3,2},{4,5},{5,4},{6,7},{7,6},{8,9},{9,8},{10,11... | collective-permute-start | bytes 1572872 | tf_op jit(solution)/shard_map/ppermute | solution.py:235
  17.2 13.4 %copy-start.1 = (f32[2,512]{1,0:T(2,128)S(1)}, f32[2,512]{1,0:T(2,128)}, u32[]{:S(2)}) copy-start(f32[2,512]{1,0:T(2,128)} %param.15) | copy-start | bytes 12292
  17.2 13.4 %copy-start.2 = (f32[2,512]{1,0:T(2,128)S(1)}, f32[2,512]{1,0:T(2,128)}, u32[]{:S(2)}) copy-start(f32[2,512]{1,0:T(2,128)} %param.16) | copy-start | bytes 12292
  17.2 13.4 %copy-start.3 = (f32[2,512]{1,0:T(2,128)S(1)}, f32[2,512]{1,0:T(2,128)}, u32[]{:S(2)}) copy-start(f32[2,512]{1,0:T(2,128)} %param.17) | copy-start | bytes 12292
  94.8 5.5 %collective-permute-start.1 = (bf16[16,16,8,128]{3,2,1,0:T(8,128)(2,1)S(1)}, bf16[16,16,8,128]{3,2,1,0:T(8,128)(2,1)S(1)}, u32[]{:S(2)}, u32[]{:S(2)}) collective-permute-start(bf16[16,16,8,128]{3,2,1,0:T(8,128)(2,1)S(1)} %all_to_all.17.source), channel_id=1, source_target_pairs={{0,1},{1,0},{2,3},{3,2},{4,5},{5,4},{6,7},{7,6},{8,9},{9,8},{10,11... | collective-permute-start | bytes 1572872 | tf_op jit(solution)/shard_map/ppermute | solution.py:266
